TPU v7x, 32 devices: a whole 2x2x4 slice. The times are simulated.
32 devices in a mesh: grp: 2 (over x), row: 16 (over z, y, core).
Axes of the slice: x: 2, y: 2, z: 4, core: 2. Of those that a mesh axis runs over, the one named last changes fastest.
Arguments:
- latent: bfloat16 [4, 16, 48, 16], P('grp', 'row'), parts along dimension 0, may hold values from -70 to 70
- w_in: bfloat16 [27, 16, 512], replicated, may hold values from -0.3125 to 0.3125
- gain_in: float32 [512], replicated, may hold values from 0.25 to 1.75
- w_query: bfloat16 [512, 512], replicated, may hold values from -0.2298097 to 0.2298097
- w_key: bfloat16 [512, 512], replicated, may hold values from -1.45840774 to 1.45840774
- w_value: bfloat16 [512, 512], replicated, may hold values from -0.25 to 0.25
- w_out: bfloat16 [512, 512], replicated, may hold values from -0.25 to 0.25
- gain_up: float32 [512], replicated, may hold values from 0.25 to 1.75
- w_up: bfloat16 [27, 512, 512], P(None, 'row'), may hold values from -0.0546875 to 0.0546875
Outputs:
- decoded: bfloat16 [4, 32, 96, 512], P('grp', 'row'), parts along dimension 0
There are 2 independent parts, one for each index of `grp`. A program takes and returns all parts, laid end to end along the dimension named above; an argument that names none is the same for every part. Nothing has to cross between parts.
All inputs are finite; a program needn't handle non-finite values.
Results may differ from a plain program's by a relative error of at most 0.015.
Values may be sent and summed in bfloat16 or wider, within the bound.
No kernel may reach another device: no remote copies, remote signals or barrier semaphores. Data moves between devices by JAX's collectives and lax.ppermute only.
A program may use at most 128 MiB of HBM per device.

v0:
```python
import functools
import math

import jax
import jax.numpy as jnp
import numpy as np
from jax import lax
from jax.experimental import pallas as pl
from jax.experimental.pallas import tpu as pltpu
from jax.sharding import PartitionSpec as P

GROUPS = 32


norm_eps = 1e-06


def extended(cells, sides, width):
    for axis, dim in sides:
        count = lax.axis_size(axis)
        ends = count - 1
        head = lax.slice_in_dim(cells, 0, width, axis=dim)
        tail = lax.slice_in_dim(cells, cells.shape[dim] - width, cells.shape[dim], axis=dim)
        cells = jnp.concatenate(
            [
                lax.ppermute(tail, axis, [(i, (i + 1) % count) for i in range(ends)]),
                cells,
                lax.ppermute(head, axis, [((i + 1) % count, i) for i in range(ends)]),
            ],
            axis=dim,
        )
    return cells


def pad_field(rimmed):
    spaced = jnp.pad(rimmed, ((0, 0), (0, 0), (1, 1), (0, 0)))
    first_frame = spaced[:1]
    return jnp.concatenate([first_frame, first_frame, spaced], axis=0)


def tap_windows(padded, frame_count, row_count, col_count):
    windows = []
    for frame_tap in range(3):
        for row_tap in range(3):
            for col_tap in range(3):
                windows.append(
                    padded[
                        frame_tap : frame_tap + frame_count,
                        row_tap : row_tap + row_count,
                        col_tap : col_tap + col_count,
                    ]
                )
    stacked = jnp.stack(windows, axis=3)
    return stacked.reshape(frame_count * row_count * col_count, -1)


def tap_products(padded, weight, frame_count, row_count, col_count):
    running = jnp.zeros((frame_count * row_count * col_count, weight.shape[2]), jnp.float32)
    for frame_tap in range(3):
        for row_tap in range(3):
            for col_tap in range(3):
                tap_index = (frame_tap * 3 + row_tap) * 3 + col_tap
                window = padded[
                    frame_tap : frame_tap + frame_count,
                    row_tap : row_tap + row_count,
                    col_tap : col_tap + col_count,
                ]
                window = window.reshape(frame_count * row_count * col_count, -1)
                running = running + jnp.dot(
                    window, weight[tap_index], preferred_element_type=jnp.float32
                )
    return running


def group_norm(volume, gain):
    grouped = volume.astype(jnp.float32).reshape(volume.shape[:3] + (GROUPS, -1))
    entry_count = (
        volume.shape[0]
        * volume.shape[1]
        * lax.axis_size("row")
        * volume.shape[2]
        * grouped.shape[4]
    )
    group_total = lax.psum(jnp.sum(grouped, axis=(0, 1, 2, 4)), "row")
    group_avg = group_total / entry_count
    centred = grouped - group_avg[:, None]
    variance = lax.psum(jnp.sum(centred * centred, axis=(0, 1, 2, 4)), "row") / entry_count
    normal_part = centred * lax.rsqrt(variance + norm_eps)[:, None]
    return normal_part.reshape(volume.shape) * gain


def per_device(latent, w_in, gain_in, w_query, w_key, w_value, w_out, gain_up, w_up):
    frame_count, row_count, col_count, _ = latent.shape
    chan_width = w_query.shape[0]
    rimmed = extended(latent, (("row", 1),), 1)
    first_out = jnp.dot(
        tap_windows(pad_field(rimmed), frame_count, row_count, col_count),
        w_in.reshape(-1, chan_width),
        preferred_element_type=jnp.float32,
    )
    first_out = first_out.astype(jnp.bfloat16).reshape(
        frame_count, row_count, col_count, chan_width
    )
    normed = group_norm(first_out, gain_in).astype(jnp.bfloat16)
    flat_rows = normed.reshape(-1, chan_width)
    queries = jnp.dot(flat_rows, w_query, preferred_element_type=jnp.float32).astype(jnp.bfloat16)
    queries = queries.reshape(frame_count, row_count * col_count, chan_width)
    score_scale = 1.0 / math.sqrt(chan_width)
    key_table = jnp.dot(flat_rows, w_key, preferred_element_type=jnp.float32).astype(jnp.bfloat16)
    value_table = jnp.dot(flat_rows, w_value, preferred_element_type=jnp.float32).astype(
        jnp.bfloat16
    )
    key_table = key_table.reshape(frame_count, row_count, col_count, chan_width)
    value_table = value_table.reshape(frame_count, row_count, col_count, chan_width)
    row_peak = jnp.full((frame_count, row_count * col_count), -jnp.inf, jnp.float32)
    denom = jnp.zeros((frame_count, row_count * col_count), jnp.float32)
    weighted = jnp.zeros((frame_count, row_count * col_count, chan_width), jnp.float32)
    scores = (
        jnp.einsum(
            "fqd,fkd->fqk",
            queries,
            lax.all_gather(key_table, "row", axis=1, tiled=True).reshape(
                frame_count, -1, chan_width
            ),
            preferred_element_type=jnp.float32,
        )
        * score_scale
    )
    new_peak = jnp.max(scores, axis=-1)
    correction = jnp.exp(row_peak - new_peak)
    expo = jnp.exp(scores - new_peak[..., None])
    denom = denom * correction + jnp.sum(expo, axis=-1)
    weighted = weighted * correction[..., None] + jnp.einsum(
        "fqk,fkd->fqd",
        expo.astype(jnp.bfloat16),
        lax.all_gather(value_table, "row", axis=1, tiled=True).reshape(frame_count, -1, chan_width),
        preferred_element_type=jnp.float32,
    )
    row_peak, denom, weighted = (new_peak, denom, weighted)
    attended = (weighted / denom[..., None]).astype(jnp.bfloat16).reshape(-1, chan_width)
    added = first_out.astype(jnp.float32).reshape(-1, chan_width) + jnp.dot(
        attended, w_out, preferred_element_type=jnp.float32
    )
    added = added.astype(jnp.bfloat16).reshape(frame_count, row_count, col_count, chan_width)
    full_up = lax.all_gather(w_up, "row", axis=1, tiled=True)
    upsampled = jnp.repeat(jnp.repeat(added, 2, axis=1), 2, axis=2)
    up_rimmed = extended(upsampled, (("row", 1),), 1)
    padded_up = pad_field(up_rimmed)
    running = tap_products(padded_up, full_up, frame_count, 2 * row_count, 2 * col_count)
    convolved = running.astype(jnp.bfloat16).reshape(
        frame_count, 2 * row_count, 2 * col_count, chan_width
    )
    return jax.nn.silu(group_norm(convolved, gain_up)).astype(jnp.bfloat16)


LANES = 128
MIB = 1024 * 1024


def lane_iota(width):
    return lax.broadcasted_iota(jnp.int32, (1, width), 1)


def swap_blocks(arrays, width):
    arrays = list(arrays)
    block = lane_iota(LANES) // width
    step = 1
    while step < len(arrays):
        low = (block & step) == 0
        for t in range(len(arrays)):
            if t & step == 0:
                a, b = arrays[t], arrays[t | step]
                arrays[t] = jnp.where(low, a, pltpu.roll(b, step * width, 1))
                arrays[t | step] = jnp.where(low, pltpu.roll(a, LANES - step * width, 1), b)
        step *= 2
    return arrays


def group_sum(row, group):
    width = row.shape[1]
    lane = lane_iota(width)
    step = 1
    while step < group:
        low = (lane & step) == 0
        row = row + jnp.where(
            low, pltpu.roll(row, width - step, 1), pltpu.roll(row, step, 1)
        )
        step *= 2
    return row


def fold_rows(block):
    return jnp.sum(block.reshape(-1, 8, block.shape[1]), axis=0)


def all_rows(part):
    return jnp.broadcast_to(jnp.sum(part, axis=0, keepdims=True), part.shape)


def pack_kernel(w_any, out_any, w_ref, out_ref, sems, out_sems):
    taps, _, chan_width = w_any.shape
    groups, devices = out_ref.shape[:2]
    share = chan_width // devices
    blocks = LANES // share
    copies, outs = [], []
    for g in range(groups):
        at = slice(g * blocks, min((g + 1) * blocks, taps))
        copies.append(pltpu.make_async_copy(w_any.at[at], w_ref.at[at], sems.at[g]))
        copies[-1].start()
    for g in range(groups):
        copies[g].wait()
        for col in range(chan_width // LANES):
            pieces = []
            for k in range(blocks):
                tap = g * blocks + k
                if tap < taps:
                    pieces.append(
                        w_ref[tap, :, col * LANES : (col + 1) * LANES].astype(jnp.float32)
                    )
                else:
                    pieces.append(jnp.zeros_like(pieces[0]))
            for d, piece in enumerate(swap_blocks(pieces, share)):
                out_ref[g, col * blocks + d] = piece.astype(out_ref.dtype)
        outs.append(
            pltpu.make_async_copy(
                out_ref.at[g], out_any.at[:, :, g * LANES : (g + 1) * LANES], out_sems.at[g]
            )
        )
        outs[-1].start()
    for copy in outs:
        copy.wait()


def mid_kernel(
    dims, near_ref, far_ref, spread_ref, w_in_ref, gain_ref, wq_ref, wk_ref, wv_ref, wo_ref, out_ref,
    x32, wide, edge, h_ref, q_ref, k_ref, v_ref,
):
    frames, rows, own, cols, zc, chan, chunk = dims
    per_frame = rows * cols
    total = frames * per_frame
    step = per_frame // 2
    per_tile = LANES // zc
    block = lane_iota(LANES) // zc
    me = lax.axis_index("row")
    order = rounds(rows // own)

    def piece(row, at):
        differs = me ^ (row // own)
        place = sum(
            ((differs >> (bit.bit_length() - 1)) & 1) << r for r, bit in enumerate(order[:-1])
        )
        return jnp.where(differs & order[-1] == 0, near_ref[place, at, :], far_ref[place, at, :])

    for f in range(frames):
        for g in range(rows // per_tile):
            tile = jnp.concatenate(
                [piece(g * per_tile + i, slice(f * zc, (f + 1) * zc)) for i in range(per_tile)], 0
            ).astype(jnp.float32)
            turned = tile.T
            for i in range(per_tile):
                at = f * per_frame + (g * per_tile + i) * cols
                x32[at : at + cols, :] = jnp.where(block == i, turned, 0.0).astype(x32.dtype)

    lane = lane_iota(edge.shape[2])
    col_tap = (lane // zc) % 3
    row_tap = (lane // zc) // 3
    blank = jnp.zeros((cols, edge.shape[2]), jnp.float32)
    col_index = lax.broadcasted_iota(jnp.int32, (cols, 1), 0)

    for f in range(frames):
        edge[f, 0:cols, :] = blank
        edge[f, (rows + 1) * cols : (rows + 2) * cols, :] = blank

        def columns(c, _):
            at = pl.multiple_of(f * per_frame + c * step, 16)
            v = jnp.dot(
                x32[pl.ds(at, step), :], spread_ref[...], preferred_element_type=jnp.float32
            )
            for k in range(step // cols):
                u = v[k * cols : (k + 1) * cols]
                before = jnp.where(col_index == 0, 0.0, pltpu.roll(u, 1, 0))
                after = jnp.where(col_index == cols - 1, 0.0, pltpu.roll(u, cols - 1, 0))
                u = jnp.where(col_tap == 0, before, jnp.where(col_tap == 2, after, u))
                edge[f, pl.ds(pl.multiple_of(c * step + (k + 1) * cols, 8), cols), :] = u
            return 0

        lax.fori_loop(0, per_frame // step, columns, 0)

        def lines(i, _):
            at = pl.multiple_of(i * cols, 8)
            above = edge[f, pl.ds(at, cols), :]
            here = edge[f, pl.ds(pl.multiple_of(at + cols, 8), cols), :]
            below = edge[f, pl.ds(pl.multiple_of(at + 2 * cols, 8), cols), :]
            v = jnp.where(row_tap == 0, above, jnp.where(row_tap == 2, below, here))
            wide[pl.ds(pl.multiple_of(f * per_frame + at, 16), cols), :] = v.astype(wide.dtype)
            return 0

        lax.fori_loop(0, rows, lines, 0, unroll=2)

    depth = wide.shape[1]

    def first(c, part):
        for f in range(frames):
            acc = None
            for dt in range(3):
                source = max(f + dt - 2, 0)
                at = pl.multiple_of(source * per_frame + c * chunk, 16)
                term = jnp.dot(
                    wide[pl.ds(at, chunk), :],
                    w_in_ref[dt * depth : (dt + 1) * depth, :],
                    preferred_element_type=jnp.float32,
                )
                acc = term if acc is None else acc + term
            acc = acc.astype(jnp.bfloat16)
            h_ref[pl.ds(pl.multiple_of(f * per_frame + c * chunk, 16), chunk), :] = acc
            part = part + fold_rows(acc.astype(jnp.float32))
        return part

    zero = jnp.zeros((8, chan), jnp.float32)
    part = lax.fori_loop(0, per_frame // chunk, first, zero)
    group = chan // GROUPS
    count = total * group
    mean = group_sum(all_rows(part), group) / count
    mean_row = mean[0:1]

    def spreadness(c, part):
        v = h_ref[pl.ds(pl.multiple_of(c * chunk, 16), chunk), :].astype(jnp.float32) - mean_row
        return part + fold_rows(v * v)

    part = lax.fori_loop(0, total // chunk, spreadness, zero)
    variance = group_sum(all_rows(part), group) / count
    scale_row = lax.rsqrt(variance + norm_eps)[0:1]
    gain_row = gain_ref[...]

    def project(c, _):
        at = pl.ds(pl.multiple_of(c * chunk, 16), chunk)
        v = h_ref[at, :].astype(jnp.float32) - mean_row
        normed = (v * scale_row * gain_row).astype(jnp.bfloat16)
        for w, o in ((wq_ref, q_ref), (wk_ref, k_ref), (wv_ref, v_ref)):
            o[at, :] = jnp.dot(normed, w[...], preferred_element_type=jnp.float32).astype(
                jnp.bfloat16
            )
        return 0

    lax.fori_loop(0, total // chunk, project, 0)
    score_scale = 1.0 / math.sqrt(chan)

    def attend(c, _):
        for f in range(frames):
            at = pl.ds(pl.multiple_of(f * per_frame + c * chunk, 16), chunk)
            span = slice(f * per_frame, (f + 1) * per_frame)
            scores = lax.dot_general(
                q_ref[at, :],
                k_ref[span, :],
                (((1,), (1,)), ((), ())),
                preferred_element_type=jnp.float32,
            )
            peak = jnp.max(scores, axis=-1, keepdims=True)
            expo = jnp.exp((scores - peak) * score_scale)
            denom = jnp.sum(expo, axis=-1, keepdims=True)
            mixed = jnp.dot(
                expo.astype(jnp.bfloat16), v_ref[span, :], preferred_element_type=jnp.float32
            )
            mixed = (mixed * (1.0 / denom)).astype(jnp.bfloat16)
            shifted = jnp.dot(mixed, wo_ref[...], preferred_element_type=jnp.float32)
            out_ref[at, :] = (h_ref[at, :].astype(jnp.float32) + shifted).astype(jnp.bfloat16)
        return 0

    lax.fori_loop(0, per_frame // chunk, attend, 0)


def up_kernel(
    dims, w_ref, x_ref, gain_ref, out_ref,
    fold_all, fold_old, fold_new, t_ref, m0_ref, m2_ref, s_old_ref, s_new_ref,
):
    frames, rows, cols, chan, share, chunk = dims
    per_frame = rows * cols
    width = 4 * share
    old_end, new_start = s_old_ref.shape[0], w_ref.shape[1] - s_new_ref.shape[0]
    lane = lane_iota(4 * width)
    phase, shift = (lane // share) % 4, lane // width
    same = lax.broadcasted_iota(jnp.int32, (share, 4 * width), 0) == lane % share
    p, q = phase // 2, phase % 2
    s_old_ref[18 * share :, :] = jnp.zeros((old_end - 18 * share, 4 * width), jnp.bfloat16)
    s_new_ref[: 18 * share - new_start, :] = jnp.zeros(
        (18 * share - new_start, 4 * width), jnp.bfloat16
    )
    spare = s_new_ref.shape[0] + new_start - 27 * share
    s_new_ref[27 * share - new_start :, :] = jnp.zeros((spare, 4 * width), jnp.bfloat16)
    for di in range(3):
        for dj in range(3):
            down = (di == 2) & (p == 1) | (di == 0) & (p == 0)
            along = (dj == 2) & (q == 1) | (dj == 0) & (q == 0)
            wanted = 2 * down.astype(jnp.int32) + along.astype(jnp.int32)
            value = jnp.where(same & (shift == wanted), 1.0, 0.0).astype(jnp.bfloat16)
            tap = (3 * di + dj) * share
            s_old_ref[tap : tap + share, :] = value
            s_old_ref[9 * share + tap : 9 * share + tap + share, :] = value
            tap += 18 * share - new_start
            s_new_ref[tap : tap + share, :] = value
    for c in range(chan // chunk):
        at = slice(c * chunk, (c + 1) * chunk)
        old = jnp.dot(w_ref[at, :old_end], s_old_ref[...], preferred_element_type=jnp.float32)
        new = jnp.dot(w_ref[at, new_start:], s_new_ref[...], preferred_element_type=jnp.float32)
        fold_old[at, :] = old.astype(jnp.bfloat16)
        fold_new[at, :] = new.astype(jnp.bfloat16)
        fold_all[at, :] = (old + new).astype(jnp.bfloat16)

    def products(c, _):
        at0 = pl.ds(pl.multiple_of(c * chunk, 16), chunk)
        at1 = pl.ds(pl.multiple_of(per_frame + c * chunk, 16), chunk)
        t_ref[at0, :] = jnp.dot(x_ref[at0, :], fold_all[...], preferred_element_type=jnp.float32)
        t_ref[at1, :] = jnp.dot(
            x_ref[at0, :], fold_old[...], preferred_element_type=jnp.float32
        ) + jnp.dot(x_ref[at1, :], fold_new[...], preferred_element_type=jnp.float32)
        return 0

    lax.fori_loop(0, per_frame // chunk, products, 0)
    lane = lane_iota(width)
    right = (lane // share) % 2 == 1
    lower = (lane // share) // 2 == 1
    col_index = lax.broadcasted_iota(jnp.int32, (cols, 1), 0)

    def beside(v):
        before = jnp.where(col_index == 0, 0.0, pltpu.roll(v, 1, 0))
        after = jnp.where(col_index == cols - 1, 0.0, pltpu.roll(v, cols - 1, 0))
        return jnp.where(right, after, before)

    blank = jnp.zeros((cols, width), jnp.float32)
    part = jnp.zeros((8, width), jnp.float32)
    for f in range(frames):
        m2_ref[f, 0:cols, :] = blank
        m2_ref[f, (rows + 1) * cols : (rows + 2) * cols, :] = blank

        def columns(i, _):
            at = pl.ds(pl.multiple_of(f * per_frame + i * cols, 8), cols)
            m0_ref[at, :] = t_ref[at, 0:width] + beside(t_ref[at, width : 2 * width])
            m2_ref[f, pl.ds(pl.multiple_of((i + 1) * cols, 8), cols), :] = t_ref[
                at, 2 * width : 3 * width
            ] + beside(t_ref[at, 3 * width : 4 * width])
            return 0

        lax.fori_loop(0, rows, columns, 0, unroll=2)

        def lines(i, part):
            at = pl.ds(pl.multiple_of(f * per_frame + i * cols, 8), cols)
            above = m2_ref[f, pl.ds(pl.multiple_of(i * cols, 8), cols), :]
            below = m2_ref[f, pl.ds(pl.multiple_of((i + 2) * cols, 8), cols), :]
            v = m0_ref[at, :] + jnp.where(lower, below, above)
            v = v.astype(jnp.bfloat16).astype(jnp.float32)
            m0_ref[at, :] = v
            return part + fold_rows(v)

        part = lax.fori_loop(0, rows, lines, part, unroll=2)

    group = chan // GROUPS
    count = frames * rows * cols * 4 * group

    def grouped(part):
        part = all_rows(part)
        part = part + pltpu.roll(part, 2 * share, 1)
        part = part + pltpu.roll(part, share, 1)
        return group_sum(part, group)

    mean_row = (grouped(part) / count)[0:1]

    def spreadness(i, part):
        v = m0_ref[pl.ds(pl.multiple_of(i * cols, 8), cols), :] - mean_row
        return part + fold_rows(v * v)

    part = lax.fori_loop(
        0, frames * rows, spreadness, jnp.zeros((8, width), jnp.float32), unroll=2
    )
    variance = grouped(part) / count
    me = lax.axis_index("row")
    gains = jnp.broadcast_to(gain_ref[...], (8, chan))
    gains = jnp.where(lane_iota(chan) // share == me, gains, 0.0)
    gains = sum(gains[:, k : k + width] for k in range(0, chan, width))
    gains = gains + pltpu.roll(gains, 2 * share, 1)
    gains = gains + pltpu.roll(gains, share, 1)
    scale_row = (lax.rsqrt(variance + norm_eps) * gains)[0:1]

    devices = out_ref.shape[0]
    own = rows // devices

    def finish(d, _):
        for f in range(frames):
            for r in range(own):
                at = pl.ds(pl.multiple_of(f * per_frame + (d * own + r) * cols, 8), cols)
                v = (m0_ref[at, :] - mean_row) * scale_row
                v = v / (1.0 + jnp.exp(-v))
                out_ref[d, (f * own + r) * cols : (f * own + r + 1) * cols, :] = v.astype(
                    out_ref.dtype
                )
        return 0

    lax.fori_loop(0, devices, finish, 0, unroll=2)


def place_kernel(share, x_ref, out_ref, line):
    devices = x_ref.shape[0]
    frames, lines, wide_cols, _ = out_ref.shape
    cols = wide_cols // 2
    own = lines // 2
    blocks = LANES // share
    for a in range(devices // blocks):
        for f in range(frames):
            for r in range(own):
                at = slice((f * own + r) * cols, (f * own + r + 1) * cols)
                pieces = swap_blocks(
                    [x_ref[a * blocks + s, at, :].astype(jnp.float32) for s in range(blocks)],
                    share,
                )
                for p in range(2):
                    slot = ((a * frames + f) * own + r) * 2 + p
                    for q in range(2):
                        line[slot, pl.ds(q, cols, stride=2), :] = pieces[2 * p + q]
                    out_ref[f, 2 * r + p, :, a * LANES : (a + 1) * LANES] = line[slot].astype(
                        out_ref.dtype
                    )


def fits(mesh, shapes):
    latent, w_query = shapes
    count = mesh.shape["row"]
    frames, own, cols, zc = latent
    chan = w_query[0]
    rows = own * count
    return (
        frames == 2
        and own == 1
        and count & (count - 1) == 0
        and chan == count * 32
        and LANES % zc == 0
        and LANES // zc == 8
        and cols % 16 == 0
        and cols <= LANES
        and rows % 8 == 0
        and (rows * cols) % 256 == 0
        and rows * cols <= 1024
    )


def call(kernel, out_shape, scratch, limit, flops, moved, spaces, out_space=pltpu.VMEM):
    return pl.pallas_call(
        kernel,
        out_shape=out_shape,
        in_specs=[pl.BlockSpec(memory_space=space) for space in spaces],
        out_specs=pl.BlockSpec(memory_space=out_space),
        scratch_shapes=scratch,
        compiler_params=pltpu.CompilerParams(vmem_limit_bytes=limit * MIB),
        cost_estimate=pl.CostEstimate(flops=flops, bytes_accessed=moved, transcendentals=0),
    )


def rounds(count):
    bits = [1]
    bit = count // 2
    while bit > 1:
        bits.append(bit)
        bit //= 2
    return bits


def everyone(cells, held):
    count = lax.axis_size("row")
    me = lax.axis_index("row")
    sent = cells[None]
    cells = lax.optimization_barrier(jnp.where(me < count, sent, 0))
    order = rounds(count)
    for bit in order:
        pairs = [(k, k ^ bit) for k in range(count)]
        if bit == order[-1]:
            cells, held = lax.optimization_barrier((cells, held))
            return cells, lax.ppermute(cells, "row", pairs), held
        other = lax.ppermute(sent, "row", pairs)
        cells = sent = jnp.concatenate([cells, other], 0)


def whole_video(latent, w_in, gain_in, w_query, w_key, w_value, w_out, gain_up, w_up):
    frames, own, cols, zc = latent.shape
    chan = w_query.shape[0]
    count = lax.axis_size("row")
    rows = own * count
    positions = frames * rows * cols
    share = chan // count
    blocks = LANES // share
    pad_taps = -(-27 // blocks) * blocks
    f32, bf16 = jnp.float32, jnp.bfloat16
    shape = jax.ShapeDtypeStruct
    chunk = 256

    cells = jnp.swapaxes(latent, 2, 3).reshape(frames * zc, cols)

    packed = call(
        pack_kernel, shape((count, w_up.shape[1], pad_taps * share), bf16),
        [
            pltpu.VMEM((pad_taps,) + w_up.shape[1:], bf16),
            pltpu.VMEM((pad_taps // blocks, count, w_up.shape[1], LANES), bf16),
            pltpu.SemaphoreType.DMA((pad_taps // blocks,)),
            pltpu.SemaphoreType.DMA((pad_taps // blocks,)),
        ],
        60,
        10**6,
        2 * 10**6,
        (pltpu.HBM,),
        pltpu.HBM,
    )(w_up)
    near, far, packed = everyone(cells, packed)
    weights = lax.all_to_all(packed, "row", 0, 0, tiled=True)
    weights = weights.reshape(chan, pad_taps * share)

    depth = 9 * zc
    spread = np.zeros((LANES, depth), np.float32)
    for k in range(LANES):
        for t in range(9):
            spread[k, t * zc + k % zc] = 1.0
    dims = (frames, rows, own, cols, zc, chan, chunk)
    added = call(
        functools.partial(mid_kernel, dims),
        shape((positions, chan), bf16),
        [
            pltpu.VMEM((positions, LANES), bf16),
            pltpu.VMEM((positions, depth), bf16),
            pltpu.VMEM((frames, (rows + 2) * cols, depth), f32),
        ]
        + [pltpu.VMEM((positions, chan), bf16)] * 4,
        28,
        7 * 10**9,
        6 * 10**6,
        (pltpu.VMEM,) * 9,
    )(
        near,
        far,
        jnp.asarray(spread, bf16),
        w_in.reshape(3 * depth, chan),
        gain_in.reshape(1, chan),
        w_query,
        w_key,
        w_value,
        w_out,
    )

    old_end = -(-18 * share // LANES) * LANES
    new_start = 18 * share // LANES * LANES
    dims = (frames, rows, cols, chan, share, chunk)
    width = 4 * share
    decoded = call(
        functools.partial(up_kernel, dims),
        shape((count, frames * own * cols, width), bf16),
        [pltpu.VMEM((chan, 4 * width), bf16)] * 3
        + [
            pltpu.VMEM((positions, 4 * width), f32),
            pltpu.VMEM((positions, width), f32),
            pltpu.VMEM((frames, (rows + 2) * cols, width), f32),
            pltpu.VMEM((old_end, 4 * width), bf16),
            pltpu.VMEM((pad_taps * share - new_start, 4 * width), bf16),
        ],
        16,
        3 * 10**9,
        5 * 10**6,
        (pltpu.VMEM,) * 3,
    )(weights, added, gain_up.reshape(1, chan))
    swapped = lax.all_to_all(decoded, "row", 0, 0, tiled=True)
    slots = (count // blocks) * frames * own * 2
    return call(
        functools.partial(place_kernel, share),
        shape((frames, 2 * own, 2 * cols, chan), bf16),
        [pltpu.VMEM((slots, 2 * cols, LANES), f32)],
        8,
        10**6,
        10**6,
        (pltpu.VMEM,),
    )(swapped)


def solution(mesh):
    def body(*args):
        whole = fits(mesh, (args[0].shape, args[3].shape))
        return (whole_video if whole else per_device)(*args)

    in_specs = (
        P("grp", "row", None, None),
        P(),
        P(),
        P(),
        P(),
        P(),
        P(),
        P(),
        P(None, "row", None),
    )
    out_specs = P("grp", "row", None, None)
    return jax.shard_map(
        body, mesh=mesh, in_specs=in_specs, out_specs=out_specs, check_vma=False
    )
```

profile of v0, /device:TPU:0, one launch (start us, length us, event | category | flops | bytes accessed | tf_op | source)
XLA Modules:
  0.0 68.4 jit_solution(6045347338374536503)
XLA Ops:
  0.0 0.5 collective-permute-start
  0.5 0.7 %broadcast_select_fusion = bf16[1,32,48]{2,1,0:T(8,128)(2,1)S(1)} fusion(bf16[1,32,48]{2,1,0:T(8,128)(2,1)} %bitcast.12, pred[]{:T(512)S(6)} %lt.3), kind=kLoop, calls=%fused_computation.3 | loop fusion | flops 1536 | bytes 6145 | tf_op jit(solution)/shard_map/jit(_where)/select_n | solution.py:569
  1.2 0.3 collective-permute-done
  1.5 4.0 %collective-permute-start.1 = (bf16[2,32,48]{2,1,0:T(8,128)(2,1)S(1)}, bf16[2,32,48]{2,1,0:T(8,128)(2,1)S(1)}, u32[]{:S(2)}, u32[]{:S(2)}) collective-permute-start(bf16[2,32,48]{2,1,0:T(8,128)(2,1)S(1)} %pad_maximum_fusion.2), channel_id=1, source_target_pairs={{0,8},{1,9},{2,10},{3,11},{4,12},{5,13},{6,14},{7,15},{8,0},{9,1},... | collective-permute-start | bytes 18440 | tf_op jit(solution)/shard_map/ppermute | solution.py:576
  5.5 1.7 %collective-permute-done.1 = bf16[2,32,48]{2,1,0:T(8,128)(2,1)S(1)} collective-permute-done((bf16[2,32,48]{2,1,0:T(8,128)(2,1)S(1)}, bf16[2,32,48]{2,1,0:T(8,128)(2,1)S(1)}, u32[]{:S(2)}, u32[]{:S(2)}) %collective-permute-start.1) | collective-permute-done | bytes 6176 | tf_op jit(solution)/shard_map/ppermute | solution.py:576
  7.3 0.0 copy-start
  7.3 0.0 copy-start.1
  7.3 0.0 copy-start.2
  7.3 0.0 copy-start.3
  7.3 0.0 copy-start.4
  7.3 0.0 copy-start.5
  7.3 2.0 %collective-permute-start.2 = (bf16[4,32,48]{2,1,0:T(8,128)(2,1)S(1)}, bf16[4,32,48]{2,1,0:T(8,128)(2,1)S(1)}, u32[]{:S(2)}, u32[]{:S(2)}) collective-permute-start(bf16[4,32,48]{2,1,0:T(8,128)(2,1)S(1)} %pad_maximum_fusion.1), channel_id=1, source_target_pairs={{0,4},{1,5},{2,6},{3,7},{4,0},{5,1},{6,2},{7,3},{8,12},{9,13},{10,... | collective-permute-start | bytes 36872 | tf_op jit(solution)/shard_map/ppermute | solution.py:576
  9.3 3.0 %shard_map.100 = bf16[16,32,896]{2,1,0:T(8,128)(2,1)} custom-call(bf16[27,32,512]{2,1,0:T(8,128)(2,1)} %w_any.1), custom_call_target="tpu_custom_call" | custom-call | flops 1000000 | bytes 2000000 | tf_op jit(solution)/shard_map/pallas_call | solution.py:595
  12.3 0.0 collective-permute-done.2
  12.3 5.3 %all-to-all-start = ((bf16[16,32,896]{2,1,0:T(8,128)(2,1)}), bf16[16,32,896]{2,1,0:T(8,128)(2,1)S(1)}, u32[]{:S(2)}, u32[]{:S(2)}) async-start(bf16[16,32,896]{2,1,0:T(8,128)(2,1)} %shard_map.100), calls=%async_computation | async-start | bytes 1835008 | tf_op jit(solution)/shard_map/all_to_all | solution.py:610
  17.7 1.9 %collective-permute-start.3 = (bf16[8,32,48]{2,1,0:T(8,128)(2,1)S(1)}, bf16[8,32,48]{2,1,0:T(8,128)(2,1)S(1)}, u32[]{:S(2)}, u32[]{:S(2)}) collective-permute-start(bf16[8,32,48]{2,1,0:T(8,128)(2,1)S(1)} %pad_maximum_fusion.near_ref), channel_id=1, source_target_pairs={{0,2},{1,3},{2,0},{3,1},{4,6},{5,7},{6,4},{7,5},{8,10},{9,11},{10,... | collective-permute-start | bytes 73736 | tf_op jit(solution)/shard_map/ppermute | solution.py:575
  19.6 8.1 %collective-permute-done.3.far_ref = bf16[8,32,48]{2,1,0:T(8,128)(2,1)S(1)} collective-permute-done((bf16[8,32,48]{2,1,0:T(8,128)(2,1)S(1)}, bf16[8,32,48]{2,1,0:T(8,128)(2,1)S(1)}, u32[]{:S(2)}, u32[]{:S(2)}) %collective-permute-start.3) | collective-permute-done | bytes 24608 | tf_op jit(solution)/shard_map/ppermute | solution.py:575
  27.7 0.0 copy-done
  27.7 0.0 copy-done.1
  27.7 0.0 copy-done.2
  27.7 0.0 copy-done.3
  27.7 0.0 copy-done.4
  27.7 0.0 copy-done.5
  27.7 0.0 copy-start.7
  27.7 0.8 %copy-done.7 = bf16[128,144]{1,0:T(8,128)(2,1)S(1)} copy-done((bf16[128,144]{1,0:T(8,128)(2,1)S(1)}, bf16[128,144]{1,0:T(8,128)(2,1)}, u32[]{:S(2)}) %copy-start.7) | copy-done | bytes 36888
  28.6 0.0 copy-start.6
  28.6 13.8 %shard_map.101.x_ref = bf16[1536,512]{1,0:T(8,128)(2,1)S(1)} custom-call(bf16[8,32,48]{2,1,0:T(8,128)(2,1)S(1)} %pad_maximum_fusion.near_ref, bf16[8,32,48]{2,1,0:T(8,128)(2,1)S(1)} %collective-permute-done.3.far_ref, bf16[128,144]{1,0:T(8,128)(2,1)S(1)} %copy-done.7, bf16[432,512]{1,0:T(8,128)(2,1)S(1)} %bitcast.8, f32[1,512]{1,0:T(1,128)S(1)} %bitcast.9, ...), custom_call_target="tpu_custom_call" | custom-call | flops 7000000000 | bytes 6000000 | tf_op jit(solution)/shard_map/pallas_call | solution.py:619
  42.3 0.0 copy-start.8
  42.3 1.2 %copy-done.8 = bf16[1536,512]{1,0:T(8,128)(2,1)} copy-done((bf16[1536,512]{1,0:T(8,128)(2,1)}, bf16[1536,512]{1,0:T(8,128)(2,1)S(1)}, u32[]{:S(2)}) %copy-start.8) | copy-done | bytes 1572888
  43.5 0.0 all-to-all-done
  43.5 0.0 copy-done.6
  43.5 0.0 copy-start.9
  43.5 1.4 %copy-done.9 = bf16[1536,512]{1,0:T(8,128)(2,1)S(1)} copy-done((bf16[1536,512]{1,0:T(8,128)(2,1)S(1)}, bf16[1536,512]{1,0:T(8,128)(2,1)}, u32[]{:S(2)}) %copy-start.9) | copy-done | bytes 1572888
  44.9 4.7 %shard_map.102 = bf16[16,96,128]{2,1,0:T(8,128)(2,1)S(1)} custom-call(bf16[512,896]{1,0:T(8,128)(2,1)S(1)} %bitcast.7, bf16[1536,512]{1,0:T(8,128)(2,1)S(1)} %copy-done.9, f32[1,512]{1,0:T(1,128)S(1)} %bitcast.10), custom_call_target="tpu_custom_call" | custom-call | flops 3000000000 | bytes 5000000 | tf_op jit(solution)/shard_map/pallas_call | solution.py:648
  49.6 17.4 %all_to_all.10.x_ref = bf16[16,96,128]{2,1,0:T(8,128)(2,1)S(1)} all-to-all(bf16[16,96,128]{2,1,0:T(8,128)(2,1)S(1)} %shard_map.102), channel_id=1, replica_groups=mesh['grp'=2,'row'=16] {'row'}, dimensions={0} | all-to-all | bytes 786432 | tf_op jit(solution)/shard_map/all_to_all | solution.py:664
  67.0 1.4 %shard_map.103 = bf16[2,2,96,512]{3,2,1,0:T(8,128)(2,1)} custom-call(bf16[16,96,128]{2,1,0:T(8,128)(2,1)S(1)} %all_to_all.10.x_ref), custom_call_target="tpu_custom_call" | custom-call | flops 1000000 | bytes 1000000 | tf_op jit(solution)/shard_map/pallas_call | solution.py:666
  (3 shorter events, 0.0 us)
Async XLA Ops:
  0.0 1.5 %collective-permute-start = (bf16[1,32,48]{2,1,0:T(8,128)(2,1)}, bf16[1,32,48]{2,1,0:T(8,128)(2,1)S(1)}, u32[]{:S(2)}, u32[]{:S(2)}) collective-permute-start(bf16[1,32,48]{2,1,0:T(8,128)(2,1)} %bitcast.11), channel_id=1, source_target_pairs={{0,1},{1,0},{2,3},{3,2},{4,5},{5,4},{6,7},{7,6},{8,9},{9,8},{10,11... | collective-permute-start | bytes 9224 | tf_op jit(solution)/shard_map/ppermute | solution.py:576
  1.5 5.7 %collective-permute-start.1 = (bf16[2,32,48]{2,1,0:T(8,128)(2,1)S(1)}, bf16[2,32,48]{2,1,0:T(8,128)(2,1)S(1)}, u32[]{:S(2)}, u32[]{:S(2)}) collective-permute-start(bf16[2,32,48]{2,1,0:T(8,128)(2,1)S(1)} %pad_maximum_fusion.2), channel_id=1, source_target_pairs={{0,8},{1,9},{2,10},{3,11},{4,12},{5,13},{6,14},{7,15},{8,0},{9,1},... | collective-permute-start | bytes 18440 | tf_op jit(solution)/shard_map/ppermute | solution.py:576
  7.3 20.4 %copy-start = (bf16[512,512]{1,0:T(8,128)(2,1)S(1)}, bf16[512,512]{1,0:T(8,128)(2,1)}, u32[]{:S(2)}) copy-start(bf16[512,512]{1,0:T(8,128)(2,1)} %wq_ref.1) | copy-start | bytes 1572868
  7.3 20.4 %copy-start.1 = (bf16[512,512]{1,0:T(8,128)(2,1)S(1)}, bf16[512,512]{1,0:T(8,128)(2,1)}, u32[]{:S(2)}) copy-start(bf16[512,512]{1,0:T(8,128)(2,1)} %wk_ref.1) | copy-start | bytes 1572868
  7.3 20.4 %copy-start.2 = (bf16[512,512]{1,0:T(8,128)(2,1)S(1)}, bf16[512,512]{1,0:T(8,128)(2,1)}, u32[]{:S(2)}) copy-start(bf16[512,512]{1,0:T(8,128)(2,1)} %wv_ref.1) | copy-start | bytes 1572868
  7.3 20.4 %copy-start.3 = (bf16[512,512]{1,0:T(8,128)(2,1)S(1)}, bf16[512,512]{1,0:T(8,128)(2,1)}, u32[]{:S(2)}) copy-start(bf16[512,512]{1,0:T(8,128)(2,1)} %wo_ref.1) | copy-start | bytes 1572868
  7.3 20.4 %copy-start.4 = (bf16[27,16,512]{2,1,0:T(8,128)(2,1)S(1)}, bf16[27,16,512]{2,1,0:T(8,128)(2,1)}, u32[]{:S(2)}) copy-start(bf16[27,16,512]{2,1,0:T(8,128)(2,1)} %param.11) | copy-start | bytes 1327108
  7.3 20.4 %copy-start.5 = (f32[512]{0:T(512)S(1)}, f32[512]{0:T(512)}, u32[]{:S(2)}) copy-start(f32[512]{0:T(512)} %param.12) | copy-start | bytes 6148
  7.3 5.0 %collective-permute-start.2 = (bf16[4,32,48]{2,1,0:T(8,128)(2,1)S(1)}, bf16[4,32,48]{2,1,0:T(8,128)(2,1)S(1)}, u32[]{:S(2)}, u32[]{:S(2)}) collective-permute-start(bf16[4,32,48]{2,1,0:T(8,128)(2,1)S(1)} %pad_maximum_fusion.1), channel_id=1, source_target_pairs={{0,4},{1,5},{2,6},{3,7},{4,0},{5,1},{6,2},{7,3},{8,12},{9,13},{10,... | collective-permute-start | bytes 36872 | tf_op jit(solution)/shard_map/ppermute | solution.py:576
  12.3 31.2 %all-to-all-start = ((bf16[16,32,896]{2,1,0:T(8,128)(2,1)}), bf16[16,32,896]{2,1,0:T(8,128)(2,1)S(1)}, u32[]{:S(2)}, u32[]{:S(2)}) async-start(bf16[16,32,896]{2,1,0:T(8,128)(2,1)} %shard_map.100), calls=%async_computation | async-start | bytes 1835008 | tf_op jit(solution)/shard_map/all_to_all | solution.py:610
  17.7 10.0 %collective-permute-start.3 = (bf16[8,32,48]{2,1,0:T(8,128)(2,1)S(1)}, bf16[8,32,48]{2,1,0:T(8,128)(2,1)S(1)}, u32[]{:S(2)}, u32[]{:S(2)}) collective-permute-start(bf16[8,32,48]{2,1,0:T(8,128)(2,1)S(1)} %pad_maximum_fusion.near_ref), channel_id=1, source_target_pairs={{0,2},{1,3},{2,0},{3,1},{4,6},{5,7},{6,4},{7,5},{8,10},{9,11},{10,... | collective-permute-start | bytes 73736 | tf_op jit(solution)/shard_map/ppermute | solution.py:575
  27.7 0.8 %copy-start.7 = (bf16[128,144]{1,0:T(8,128)(2,1)S(1)}, bf16[128,144]{1,0:T(8,128)(2,1)}, u32[]{:S(2)}) copy-start(bf16[128,144]{1,0:T(8,128)(2,1)} %constant.11.clone.spread_ref) | copy-start | bytes 110596
  28.6 14.9 %copy-start.6 = (f32[512]{0:T(512)S(1)}, f32[512]{0:T(512)}, u32[]{:S(2)}) copy-start(f32[512]{0:T(512)} %param.17) | copy-start | bytes 6148
  42.3 1.2 %copy-start.8 = (bf16[1536,512]{1,0:T(8,128)(2,1)}, bf16[1536,512]{1,0:T(8,128)(2,1)S(1)}, u32[]{:S(2)}) copy-start(bf16[1536,512]{1,0:T(8,128)(2,1)S(1)} %shard_map.101.x_ref) | copy-start | bytes 4718596
  43.5 1.4 %copy-start.9 = (bf16[1536,512]{1,0:T(8,128)(2,1)S(1)}, bf16[1536,512]{1,0:T(8,128)(2,1)}, u32[]{:S(2)}) copy-start(bf16[1536,512]{1,0:T(8,128)(2,1)} %copy-done.8) | copy-start | bytes 4718596
where the time goes:
time: 68.8 us; the launch traced here: 68.4 us
  Pallas kernels  22.8 us (33%)
  blocking collectives  17.4 us (25%)
  starting transfers between devices  13.7 us (20%)
  waiting for transfers between devices  10.1 us (15%)
  local copies, waits for them, and re-layouts  3.44 us (5%)
  other arithmetic  0.74 us (1%)
    all_to_all x1, blocking collectives, whole_video(): swapped = lax.all_to_all(decoded, 'row', 0, 0, tiled=True)  17.4 us
    pallas_call x1, Pallas kernels, whole_video(): call(functools.partial(mid_kernel, dims), shape((positions, chan), bf16),...  13.8 us
    ppermute x1, waiting for transfers between devices, everyone(): return (cells, lax.ppermute(cells, 'row', pairs), held)  8.07 us
    ppermute x3, starting transfers between devices, everyone(): other = lax.ppermute(sent, 'row', pairs)  6.45 us
    all_to_all x1, starting transfers between devices, whole_video(): weights = lax.all_to_all(packed, 'row', 0, 0, tiled=True)  5.33 us
    pallas_call x1, Pallas kernels, whole_video(): call(functools.partial(up_kernel, dims), shape((count, frames * own * col...  4.67 us
    unnamed x20, local copies, waits for them, and re-layouts  3.44 us
    pallas_call x1, Pallas kernels, whole_video(): call(pack_kernel, shape((count, w_up.shape[1], pad_taps * share), bf16),...  2.99 us
  transfers between devices with their start and end apart: 5, of which 3 were waited for; matrix products, arithmetic and copies ran while one was open for 1% of the time, Pallas kernels for 24%

commit v1 on v0

--- a/solution.py
+++ b/solution.py
@@ -197,28 +197,48 @@
     return jnp.broadcast_to(jnp.sum(part, axis=0, keepdims=True), part.shape)
 
 
+def tap_tiles(taps, blocks):
+    whole, rest = taps // blocks, taps % blocks
+    tiles = [[(h, t * blocks + k) for k in range(blocks)] for h in range(2) for t in range(whole)]
+    tail = []
+    for h in range(2):
+        tail += [(h, whole * blocks + k) for k in range(rest)]
+        tail += [None] * (blocks // 2 - rest)
+    return tiles + [tail]
+
+
 def pack_kernel(w_any, out_any, w_ref, out_ref, sems, out_sems):
-    taps, _, chan_width = w_any.shape
-    groups, devices = out_ref.shape[:2]
-    share = chan_width // devices
+    taps, _, width = w_ref.shape
+    groups, devices, depth, _ = out_ref.shape
+    share = width // devices
     blocks = LANES // share
+    first = pl.multiple_of(lax.axis_index("grp") * width, LANES)
     copies, outs = [], []
-    for g in range(groups):
+    for g in range(sems.shape[0]):
         at = slice(g * blocks, min((g + 1) * blocks, taps))
-        copies.append(pltpu.make_async_copy(w_any.at[at], w_ref.at[at], sems.at[g]))
+        copies.append(
+            pltpu.make_async_copy(
+                w_any.at[at, :, pl.ds(first, width)], w_ref.at[at], sems.at[g]
+            )
+        )
         copies[-1].start()
-    for g in range(groups):
-        copies[g].wait()
-        for col in range(chan_width // LANES):
-            pieces = []
-            for k in range(blocks):
-                tap = g * blocks + k
-                if tap < taps:
-                    pieces.append(
-                        w_ref[tap, :, col * LANES : (col + 1) * LANES].astype(jnp.float32)
-                    )
-                else:
-                    pieces.append(jnp.zeros_like(pieces[0]))
+    tiles = tap_tiles(taps, blocks)
+    loaded = 0
+    for g in sorted(range(groups), key=lambda g: max(unit[1] for unit in tiles[g] if unit)):
+        while loaded * blocks <= max(unit[1] for unit in tiles[g] if unit):
+            copies[loaded].wait()
+            loaded += 1
+        for col in range(width // LANES):
+            pieces = [
+                jnp.zeros((depth, LANES), jnp.float32)
+                if unit is None
+                else w_ref[
+                    unit[1],
+                    unit[0] * depth : (unit[0] + 1) * depth,
+                    col * LANES : (col + 1) * LANES,
+                ].astype(jnp.float32)
+                for unit in tiles[g]
+            ]
             for d, piece in enumerate(swap_blocks(pieces, share)):
                 out_ref[g, col * blocks + d] = piece.astype(out_ref.dtype)
         outs.append(
@@ -232,9 +252,13 @@
 
 
 def mid_kernel(
-    dims, near_ref, far_ref, spread_ref, w_in_ref, gain_ref, wq_ref, wk_ref, wv_ref, wo_ref, out_ref,
-    x32, wide, edge, h_ref, q_ref, k_ref, v_ref,
+    dims, near_ref, far_ref, spread_ref, w_in_ref, gain_ref, wq_any, wk_any, wv_any, wo_any, out_ref,
+    x32, wide, edge, h_ref, q_ref, k_ref, v_ref, wq_ref, wk_ref, wv_ref, wo_ref, sems,
 ):
+    pairs = ((wq_any, wq_ref), (wk_any, wk_ref), (wv_any, wv_ref), (wo_any, wo_ref))
+    loads = [pltpu.make_async_copy(a, b, sems.at[k]) for k, (a, b) in enumerate(pairs)]
+    for load in loads:
+        load.start()
     frames, rows, own, cols, zc, chan, chunk = dims
     per_frame = rows * cols
     total = frames * per_frame
@@ -299,25 +323,25 @@
 
     depth = wide.shape[1]
 
-    def first(c, part):
+    def first(part):
         for f in range(frames):
             acc = None
             for dt in range(3):
                 source = max(f + dt - 2, 0)
-                at = pl.multiple_of(source * per_frame + c * chunk, 16)
+                at = source * per_frame
                 term = jnp.dot(
-                    wide[pl.ds(at, chunk), :],
+                    wide[at : at + per_frame, :],
                     w_in_ref[dt * depth : (dt + 1) * depth, :],
                     preferred_element_type=jnp.float32,
                 )
                 acc = term if acc is None else acc + term
             acc = acc.astype(jnp.bfloat16)
-            h_ref[pl.ds(pl.multiple_of(f * per_frame + c * chunk, 16), chunk), :] = acc
+            h_ref[slice(f * per_frame, (f + 1) * per_frame), :] = acc
             part = part + fold_rows(acc.astype(jnp.float32))
         return part
 
     zero = jnp.zeros((8, chan), jnp.float32)
-    part = lax.fori_loop(0, per_frame // chunk, first, zero)
+    part = first(zero)
     group = chan // GROUPS
     count = total * group
     mean = group_sum(all_rows(part), group) / count
@@ -331,6 +355,9 @@
     variance = group_sum(all_rows(part), group) / count
     scale_row = lax.rsqrt(variance + norm_eps)[0:1]
     gain_row = gain_ref[...]
+
+    for load in loads:
+        load.wait()
 
     def project(c, _):
         at = pl.ds(pl.multiple_of(c * chunk, 16), chunk)
@@ -342,83 +369,92 @@
             )
         return 0
 
-    lax.fori_loop(0, total // chunk, project, 0)
+    lax.fori_loop(0, total // chunk, project, 0, unroll=total // chunk)
     score_scale = 1.0 / math.sqrt(chan)
 
-    def attend(c, _):
-        for f in range(frames):
-            at = pl.ds(pl.multiple_of(f * per_frame + c * chunk, 16), chunk)
-            span = slice(f * per_frame, (f + 1) * per_frame)
-            scores = lax.dot_general(
-                q_ref[at, :],
-                k_ref[span, :],
-                (((1,), (1,)), ((), ())),
-                preferred_element_type=jnp.float32,
-            )
-            peak = jnp.max(scores, axis=-1, keepdims=True)
-            expo = jnp.exp((scores - peak) * score_scale)
-            denom = jnp.sum(expo, axis=-1, keepdims=True)
-            mixed = jnp.dot(
-                expo.astype(jnp.bfloat16), v_ref[span, :], preferred_element_type=jnp.float32
-            )
-            mixed = (mixed * (1.0 / denom)).astype(jnp.bfloat16)
-            shifted = jnp.dot(mixed, wo_ref[...], preferred_element_type=jnp.float32)
-            out_ref[at, :] = (h_ref[at, :].astype(jnp.float32) + shifted).astype(jnp.bfloat16)
-        return 0
-
-    lax.fori_loop(0, per_frame // chunk, attend, 0)
-
-
-def up_kernel(
-    dims, w_ref, x_ref, gain_ref, out_ref,
-    fold_all, fold_old, fold_new, t_ref, m0_ref, m2_ref, s_old_ref, s_new_ref,
-):
-    frames, rows, cols, chan, share, chunk = dims
-    per_frame = rows * cols
-    width = 4 * share
-    old_end, new_start = s_old_ref.shape[0], w_ref.shape[1] - s_new_ref.shape[0]
-    lane = lane_iota(4 * width)
-    phase, shift = (lane // share) % 4, lane // width
-    same = lax.broadcasted_iota(jnp.int32, (share, 4 * width), 0) == lane % share
-    p, q = phase // 2, phase % 2
-    s_old_ref[18 * share :, :] = jnp.zeros((old_end - 18 * share, 4 * width), jnp.bfloat16)
-    s_new_ref[: 18 * share - new_start, :] = jnp.zeros(
-        (18 * share - new_start, 4 * width), jnp.bfloat16
-    )
-    spare = s_new_ref.shape[0] + new_start - 27 * share
-    s_new_ref[27 * share - new_start :, :] = jnp.zeros((spare, 4 * width), jnp.bfloat16)
+    for f in range(frames):
+        at = slice(f * per_frame, (f + 1) * per_frame)
+        span = slice(f * per_frame, (f + 1) * per_frame)
+        scores = lax.dot_general(
+            q_ref[at, :],
+            k_ref[span, :],
+            (((1,), (1,)), ((), ())),
+            preferred_element_type=jnp.float32,
+        )
+        peak = jnp.max(scores, axis=-1, keepdims=True)
+        expo = jnp.exp2((scores - peak) * (score_scale * math.log2(math.e)))
+        denom = jnp.sum(expo, axis=-1, keepdims=True)
+        mixed = jnp.dot(
+            expo.astype(jnp.bfloat16), v_ref[span, :], preferred_element_type=jnp.float32
+        )
+        mixed = (mixed * (1.0 / denom)).astype(jnp.bfloat16)
+        shifted = jnp.dot(mixed, wo_ref[...], preferred_element_type=jnp.float32)
+        out_ref[at, :] = (h_ref[at, :].astype(jnp.float32) + shifted).astype(jnp.bfloat16)
+
+
+def fold_taps(w_ref, all_ref, new_ref, s_all, s_new, share):
+    blocks = LANES // share
+    width = s_all.shape[1]
+    whole = 27 // blocks
+    lane = lane_iota(width)
+    inner, shift = (lane // share) % blocks, lane // LANES
+    later, p, q = inner // 4 == 1, (inner // 2) % 2, inner % 2
+    same = lax.broadcasted_iota(jnp.int32, (share, width), 0) == lane % share
+    s_all[whole * LANES :, :] = jnp.zeros((2 * LANES, width), s_all.dtype)
+    s_new[...] = jnp.zeros_like(s_new)
     for di in range(3):
         for dj in range(3):
             down = (di == 2) & (p == 1) | (di == 0) & (p == 0)
             along = (dj == 2) & (q == 1) | (dj == 0) & (q == 0)
             wanted = 2 * down.astype(jnp.int32) + along.astype(jnp.int32)
-            value = jnp.where(same & (shift == wanted), 1.0, 0.0).astype(jnp.bfloat16)
-            tap = (3 * di + dj) * share
-            s_old_ref[tap : tap + share, :] = value
-            s_old_ref[9 * share + tap : 9 * share + tap + share, :] = value
-            tap += 18 * share - new_start
-            s_new_ref[tap : tap + share, :] = value
-    for c in range(chan // chunk):
-        at = slice(c * chunk, (c + 1) * chunk)
-        old = jnp.dot(w_ref[at, :old_end], s_old_ref[...], preferred_element_type=jnp.float32)
-        new = jnp.dot(w_ref[at, new_start:], s_new_ref[...], preferred_element_type=jnp.float32)
-        fold_old[at, :] = old.astype(jnp.bfloat16)
-        fold_new[at, :] = new.astype(jnp.bfloat16)
-        fold_all[at, :] = (old + new).astype(jnp.bfloat16)
-
-    def products(c, _):
-        at0 = pl.ds(pl.multiple_of(c * chunk, 16), chunk)
-        at1 = pl.ds(pl.multiple_of(per_frame + c * chunk, 16), chunk)
-        t_ref[at0, :] = jnp.dot(x_ref[at0, :], fold_all[...], preferred_element_type=jnp.float32)
-        t_ref[at1, :] = jnp.dot(
-            x_ref[at0, :], fold_old[...], preferred_element_type=jnp.float32
-        ) + jnp.dot(x_ref[at1, :], fold_new[...], preferred_element_type=jnp.float32)
-        return 0
-
-    lax.fori_loop(0, per_frame // chunk, products, 0)
+            fits_here = same & (shift == wanted)
+            both, early, late = (
+                jnp.where(v, 1.0, 0.0).astype(s_all.dtype)
+                for v in (fits_here, fits_here & ~later, fits_here & later)
+            )
+            for dt in range(3):
+                tap = 9 * dt + 3 * di + dj
+                if tap < whole * blocks:
+                    s_all[tap * share : (tap + 1) * share, :] = early if dt == 2 else both
+                    if dt == 2:
+                        at = (tap - (whole - 1) * blocks) * share
+                        s_new[at : at + share, :] = late
+                else:
+                    for h in range(2):
+                        at = h * (LANES + LANES // 2) + (tap - whole * blocks) * share
+                        s_all[whole * LANES + at : whole * LANES + at + share, :] = early
+                        s_new[LANES + at : LANES + at + share, :] = late
+    tail = slice(2 * whole * LANES, (2 * whole + 1) * LANES)
+    for h in range(2):
+        main = slice(h * whole * LANES, (h + 1) * whole * LANES)
+        last = slice(((h + 1) * whole - 1) * LANES, (h + 1) * whole * LANES)
+        side = slice((whole + h) * LANES, (whole + h + 1) * LANES)
+        new_side = slice((1 + h) * LANES, (2 + h) * LANES)
+        for (lanes, s_ref, rows, side_rows), to_ref in (
+            ((main, s_all, slice(0, whole * LANES), side), all_ref),
+            ((last, s_new, slice(0, LANES), new_side), new_ref),
+        ):
+            v = jnp.dot(w_ref[:, lanes], s_ref[rows, :], preferred_element_type=jnp.float32)
+            v += jnp.dot(w_ref[:, tail], s_ref[side_rows, :], preferred_element_type=jnp.float32)
+            v = v.astype(to_ref.dtype)
+            for k in range(v.shape[0] // share):
+                at = (2 * k + h) * share
+                to_ref[at : at + share, :] = v[k * share : (k + 1) * share]
+
+
+def up_video(dims, x_ref, all_ref, new_ref, gain_ref, t_ref, m0_ref, m2_ref, store):
+    rows, cols, chan, share, _ = dims
+    per_frame = rows * cols
+    width = LANES
+
+    t_ref[...] = jnp.dot(
+        x_ref[0:per_frame, :], all_ref[...], preferred_element_type=jnp.float32
+    ) + jnp.dot(
+        x_ref[per_frame : 2 * per_frame, :], new_ref[...], preferred_element_type=jnp.float32
+    )
     lane = lane_iota(width)
     right = (lane // share) % 2 == 1
-    lower = (lane // share) // 2 == 1
+    lower = (lane // (2 * share)) % 2 == 1
     col_index = lax.broadcasted_iota(jnp.int32, (cols, 1), 0)
 
     def beside(v):
@@ -427,40 +463,41 @@
         return jnp.where(right, after, before)
 
     blank = jnp.zeros((cols, width), jnp.float32)
-    part = jnp.zeros((8, width), jnp.float32)
-    for f in range(frames):
-        m2_ref[f, 0:cols, :] = blank
-        m2_ref[f, (rows + 1) * cols : (rows + 2) * cols, :] = blank
-
-        def columns(i, _):
-            at = pl.ds(pl.multiple_of(f * per_frame + i * cols, 8), cols)
-            m0_ref[at, :] = t_ref[at, 0:width] + beside(t_ref[at, width : 2 * width])
-            m2_ref[f, pl.ds(pl.multiple_of((i + 1) * cols, 8), cols), :] = t_ref[
-                at, 2 * width : 3 * width
-            ] + beside(t_ref[at, 3 * width : 4 * width])
-            return 0
-
-        lax.fori_loop(0, rows, columns, 0, unroll=2)
-
-        def lines(i, part):
-            at = pl.ds(pl.multiple_of(f * per_frame + i * cols, 8), cols)
-            above = m2_ref[f, pl.ds(pl.multiple_of(i * cols, 8), cols), :]
-            below = m2_ref[f, pl.ds(pl.multiple_of((i + 2) * cols, 8), cols), :]
-            v = m0_ref[at, :] + jnp.where(lower, below, above)
-            v = v.astype(jnp.bfloat16).astype(jnp.float32)
-            m0_ref[at, :] = v
-            return part + fold_rows(v)
-
-        part = lax.fori_loop(0, rows, lines, part, unroll=2)
-
+    m2_ref[0:cols, :] = blank
+    m2_ref[(rows + 1) * cols : (rows + 2) * cols, :] = blank
+
+    def columns(i, _):
+        at = pl.ds(pl.multiple_of(i * cols, 8), cols)
+        m0_ref[at, :] = t_ref[at, 0:width] + beside(t_ref[at, width : 2 * width])
+        m2_ref[pl.ds(pl.multiple_of((i + 1) * cols, 8), cols), :] = t_ref[
+            at, 2 * width : 3 * width
+        ] + beside(t_ref[at, 3 * width : 4 * width])
+        return 0
+
+    lax.fori_loop(0, rows, columns, 0, unroll=2)
+
+    def lines(i, part):
+        at = pl.ds(pl.multiple_of(i * cols, 8), cols)
+        above = m2_ref[at, :]
+        below = m2_ref[pl.ds(pl.multiple_of((i + 2) * cols, 8), cols), :]
+        v = m0_ref[at, :] + jnp.where(lower, below, above)
+        v = v.astype(jnp.bfloat16).astype(jnp.float32)
+        m0_ref[at, :] = v
+        return part + fold_rows(v)
+
+    part = lax.fori_loop(0, rows, lines, jnp.zeros((8, width), jnp.float32), unroll=2)
     group = chan // GROUPS
-    count = frames * rows * cols * 4 * group
+    count = 2 * rows * cols * 4 * group
+
+    def over_blocks(row):
+        step = share
+        while step < width:
+            row = row + pltpu.roll(row, step, 1)
+            step *= 2
+        return row
 
     def grouped(part):
-        part = all_rows(part)
-        part = part + pltpu.roll(part, 2 * share, 1)
-        part = part + pltpu.roll(part, share, 1)
-        return group_sum(part, group)
+        return group_sum(over_blocks(all_rows(part)), group)
 
     mean_row = (grouped(part) / count)[0:1]
 
@@ -468,56 +505,67 @@
         v = m0_ref[pl.ds(pl.multiple_of(i * cols, 8), cols), :] - mean_row
         return part + fold_rows(v * v)
 
-    part = lax.fori_loop(
-        0, frames * rows, spreadness, jnp.zeros((8, width), jnp.float32), unroll=2
-    )
+    part = lax.fori_loop(0, rows, spreadness, jnp.zeros((8, width), jnp.float32), unroll=2)
     variance = grouped(part) / count
-    me = lax.axis_index("row")
+    me = lax.axis_index("grp") * lax.axis_size("row") + lax.axis_index("row")
     gains = jnp.broadcast_to(gain_ref[...], (8, chan))
     gains = jnp.where(lane_iota(chan) // share == me, gains, 0.0)
-    gains = sum(gains[:, k : k + width] for k in range(0, chan, width))
-    gains = gains + pltpu.roll(gains, 2 * share, 1)
-    gains = gains + pltpu.roll(gains, share, 1)
+    gains = over_blocks(sum(gains[:, k : k + width] for k in range(0, chan, width)))
     scale_row = (lax.rsqrt(variance + norm_eps) * gains)[0:1]
 
-    devices = out_ref.shape[0]
-    own = rows // devices
-
     def finish(d, _):
-        for f in range(frames):
-            for r in range(own):
-                at = pl.ds(pl.multiple_of(f * per_frame + (d * own + r) * cols, 8), cols)
-                v = (m0_ref[at, :] - mean_row) * scale_row
-                v = v / (1.0 + jnp.exp(-v))
-                out_ref[d, (f * own + r) * cols : (f * own + r + 1) * cols, :] = v.astype(
-                    out_ref.dtype
-                )
+        at = pl.ds(pl.multiple_of(d * cols, 8), cols)
+        v = (m0_ref[at, :] - mean_row) * scale_row
+        store(d, v / (1.0 + jnp.exp(-v)))
         return 0
 
-    lax.fori_loop(0, devices, finish, 0, unroll=2)
+    lax.fori_loop(0, rows, finish, 0, unroll=2)
+
+
+def near_kernel(
+    dims, w_ref, x_ref, gain_ref, out_ref, all_ref, new_ref, t_ref, m0_ref, m2_ref, s_all, s_new
+):
+    fold_taps(w_ref, all_ref, new_ref, s_all, s_new, dims[3])
+
+    def store(d, v):
+        out_ref[d] = v.astype(out_ref.dtype)
+
+    up_video(dims, x_ref, all_ref, new_ref, gain_ref, t_ref, m0_ref, m2_ref, store)
+
+
+def far_kernel(
+    dims, near_ref, x_ref, all_ref, new_ref, gain_ref, out_ref, t_ref, m0_ref, m2_ref
+):
+    rows = dims[0]
+    video = lax.axis_index("row") % 2
+
+    def keep(d, _):
+        out_ref[video * rows + d] = near_ref[d]
+        return 0
+
+    lax.fori_loop(0, rows, keep, 0, unroll=4)
+
+    def store(d, v):
+        out_ref[(1 - video) * rows + d] = v.astype(out_ref.dtype)
+
+    up_video(dims, x_ref, all_ref, new_ref, gain_ref, t_ref, m0_ref, m2_ref, store)
 
 
 def place_kernel(share, x_ref, out_ref, line):
     devices = x_ref.shape[0]
-    frames, lines, wide_cols, _ = out_ref.shape
-    cols = wide_cols // 2
-    own = lines // 2
     blocks = LANES // share
+    cols = x_ref.shape[1]
     for a in range(devices // blocks):
-        for f in range(frames):
-            for r in range(own):
-                at = slice((f * own + r) * cols, (f * own + r + 1) * cols)
-                pieces = swap_blocks(
-                    [x_ref[a * blocks + s, at, :].astype(jnp.float32) for s in range(blocks)],
-                    share,
-                )
-                for p in range(2):
-                    slot = ((a * frames + f) * own + r) * 2 + p
-                    for q in range(2):
-                        line[slot, pl.ds(q, cols, stride=2), :] = pieces[2 * p + q]
-                    out_ref[f, 2 * r + p, :, a * LANES : (a + 1) * LANES] = line[slot].astype(
-                        out_ref.dtype
-                    )
+        pieces = swap_blocks(
+            [x_ref[a * blocks + k].astype(jnp.float32) for k in range(blocks)], share
+        )
+        for half in range(blocks // 2):
+            slot = a * (blocks // 2) + half
+            for q in range(2):
+                line[slot, pl.ds(q, cols, stride=2), :] = pieces[2 * half + q]
+            out_ref[half // 2, half % 2, :, a * LANES : (a + 1) * LANES] = line[slot].astype(
+                out_ref.dtype
+            )
 
 
 def fits(mesh, shapes):
@@ -526,16 +574,19 @@
     frames, own, cols, zc = latent
     chan = w_query[0]
     rows = own * count
+    share = chan // (2 * count)
     return (
-        frames == 2
+        mesh.shape["grp"] == 2
+        and frames == 2
         and own == 1
+        and count >= 8
         and count & (count - 1) == 0
-        and chan == count * 32
-        and LANES % zc == 0
-        and LANES // zc == 8
+        and share == 16
+        and chan == 2 * count * share
+        and chan == GROUPS * share
+        and zc == 16
         and cols % 16 == 0
         and cols <= LANES
-        and rows % 8 == 0
         and (rows * cols) % 256 == 0
         and rows * cols <= 1024
     )
@@ -546,7 +597,7 @@
         kernel,
         out_shape=out_shape,
         in_specs=[pl.BlockSpec(memory_space=space) for space in spaces],
-        out_specs=pl.BlockSpec(memory_space=out_space),
+        out_specs=jax.tree.map(lambda space: pl.BlockSpec(memory_space=space), out_space),
         scratch_shapes=scratch,
         compiler_params=pltpu.CompilerParams(vmem_limit_bytes=limit * MIB),
         cost_estimate=pl.CostEstimate(flops=flops, bytes_accessed=moved, transcendentals=0),
@@ -565,10 +616,24 @@
 def everyone(cells, held):
     count = lax.axis_size("row")
     me = lax.axis_index("row")
+    grp = lax.axis_index("grp")
     sent = cells[None]
-    cells = lax.optimization_barrier(jnp.where(me < count, sent, 0))
+    own = lax.optimization_barrier(jnp.where(me < count, sent, 0))
+    to_one, to_two = [], []
+    for g in range(2):
+        for k in range(count):
+            here = g * count + k
+            if g == k % 2:
+                to_one.append((here, (1 - g) * count + k))
+            else:
+                to_one.append((here, g * count + (k ^ 1)))
+                to_two.append((here, (1 - g) * count + (k ^ 1)))
+    one = lax.ppermute(sent, ("grp", "row"), to_one)
+    two = lax.ppermute(sent, ("grp", "row"), to_two)
+    mine = grp == me % 2
+    cells = sent = jnp.concatenate([jnp.where(mine, own, one), jnp.where(mine, one, two)], 0)
     order = rounds(count)
-    for bit in order:
+    for bit in order[1:]:
         pairs = [(k, k ^ bit) for k in range(count)]
         if bit == order[-1]:
             cells, held = lax.optimization_barrier((cells, held))
@@ -583,9 +648,9 @@
     count = lax.axis_size("row")
     rows = own * count
     positions = frames * rows * cols
-    share = chan // count
+    share = chan // (2 * count)
     blocks = LANES // share
-    pad_taps = -(-27 // blocks) * blocks
+    tiles = len(tap_tiles(27, blocks))
     f32, bf16 = jnp.float32, jnp.bfloat16
     shape = jax.ShapeDtypeStruct
     chunk = 256
@@ -593,22 +658,23 @@
     cells = jnp.swapaxes(latent, 2, 3).reshape(frames * zc, cols)
 
     packed = call(
-        pack_kernel, shape((count, w_up.shape[1], pad_taps * share), bf16),
+        pack_kernel,
+        shape((count, share, tiles * LANES), bf16),
         [
-            pltpu.VMEM((pad_taps,) + w_up.shape[1:], bf16),
-            pltpu.VMEM((pad_taps // blocks, count, w_up.shape[1], LANES), bf16),
-            pltpu.SemaphoreType.DMA((pad_taps // blocks,)),
-            pltpu.SemaphoreType.DMA((pad_taps // blocks,)),
+            pltpu.VMEM((27, 2 * share, count * share), bf16),
+            pltpu.VMEM((tiles, count, share, LANES), bf16),
+            pltpu.SemaphoreType.DMA((-(-27 // blocks),)),
+            pltpu.SemaphoreType.DMA((tiles,)),
         ],
-        60,
+        8,
         10**6,
         2 * 10**6,
         (pltpu.HBM,),
         pltpu.HBM,
-    )(w_up)
+    )(pltpu.with_memory_space_constraint(w_up, pltpu.HBM))
     near, far, packed = everyone(cells, packed)
     weights = lax.all_to_all(packed, "row", 0, 0, tiled=True)
-    weights = weights.reshape(chan, pad_taps * share)
+    weights = weights.reshape(chan // 2, tiles * LANES)
 
     depth = 9 * zc
     spread = np.zeros((LANES, depth), np.float32)
@@ -616,7 +682,7 @@
         for t in range(9):
             spread[k, t * zc + k % zc] = 1.0
     dims = (frames, rows, own, cols, zc, chan, chunk)
-    added = call(
+    middle = call(
         functools.partial(mid_kernel, dims),
         shape((positions, chan), bf16),
         [
@@ -624,49 +690,61 @@
             pltpu.VMEM((positions, depth), bf16),
             pltpu.VMEM((frames, (rows + 2) * cols, depth), f32),
         ]
-        + [pltpu.VMEM((positions, chan), bf16)] * 4,
+        + [pltpu.VMEM((positions, chan), bf16)] * 4
+        + [pltpu.VMEM((chan, chan), bf16)] * 4
+        + [pltpu.SemaphoreType.DMA((4,))],
         28,
         7 * 10**9,
         6 * 10**6,
-        (pltpu.VMEM,) * 9,
-    )(
+        (pltpu.VMEM,) * 5 + (pltpu.HBM,) * 4,
+    )
+    added = middle(
         near,
         far,
         jnp.asarray(spread, bf16),
         w_in.reshape(3 * depth, chan),
         gain_in.reshape(1, chan),
-        w_query,
-        w_key,
-        w_value,
-        w_out,
-    )
-
-    old_end = -(-18 * share // LANES) * LANES
-    new_start = 18 * share // LANES * LANES
-    dims = (frames, rows, cols, chan, share, chunk)
-    width = 4 * share
+        *(
+            pltpu.with_memory_space_constraint(w, pltpu.HBM)
+            for w in (w_query, w_key, w_value, w_out)
+        ),
+    )
+
+    dims = (rows, cols, chan, share, chunk)
+    width = 4 * LANES
+    gain = gain_up.reshape(1, chan)
+    fields = [
+        pltpu.VMEM((rows * cols, width), f32),
+        pltpu.VMEM((rows * cols, LANES), f32),
+        pltpu.VMEM(((rows + 2) * cols, LANES), f32),
+    ]
+    fold = shape((chan, width), bf16)
+    first = call(
+        functools.partial(near_kernel, dims),
+        (shape((count, cols, LANES), bf16), fold, fold),
+        fields + [pltpu.VMEM((5 * LANES, width), bf16), pltpu.VMEM((3 * LANES, width), bf16)],
+        16,
+        2 * 10**9,
+        3 * 10**6,
+        (pltpu.VMEM,) * 3,
+        (pltpu.VMEM,) * 3,
+    )
+    near_out, fold_all, fold_new = first(weights, added, gain)
+    other = lax.ppermute(added, "row", [(k, k ^ 1) for k in range(count)])
     decoded = call(
-        functools.partial(up_kernel, dims),
-        shape((count, frames * own * cols, width), bf16),
-        [pltpu.VMEM((chan, 4 * width), bf16)] * 3
-        + [
-            pltpu.VMEM((positions, 4 * width), f32),
-            pltpu.VMEM((positions, width), f32),
-            pltpu.VMEM((frames, (rows + 2) * cols, width), f32),
-            pltpu.VMEM((old_end, 4 * width), bf16),
-            pltpu.VMEM((pad_taps * share - new_start, 4 * width), bf16),
-        ],
+        functools.partial(far_kernel, dims),
+        shape((2 * count, cols, LANES), bf16),
+        fields,
         16,
-        3 * 10**9,
-        5 * 10**6,
-        (pltpu.VMEM,) * 3,
-    )(weights, added, gain_up.reshape(1, chan))
-    swapped = lax.all_to_all(decoded, "row", 0, 0, tiled=True)
-    slots = (count // blocks) * frames * own * 2
+        2 * 10**9,
+        3 * 10**6,
+        (pltpu.VMEM,) * 5,
+    )(near_out, other, fold_all, fold_new, gain)
+    swapped = lax.all_to_all(decoded, ("grp", "row"), 0, 0, tiled=True)
     return call(
         functools.partial(place_kernel, share),
         shape((frames, 2 * own, 2 * cols, chan), bf16),
-        [pltpu.VMEM((slots, 2 * cols, LANES), f32)],
+        [pltpu.VMEM((2 * count // 2, 2 * cols, LANES), f32)],
         8,
         10**6,
         10**6,

time: 68.8 us -> 74.8 us (1.087)
  blocking collectives: 17.4 us -> 36.1 us
  waiting for transfers between devices: 10.1 us -> 5.64 us
  local copies, waits for them, and re-layouts: 3.44 us -> 0.02 us
  starting transfers between devices: 13.7 us -> 11 us
  Pallas kernels: 22.8 us -> 21 us
    all_to_all x1 -> x2, blocking collectives: 17.4 us -> 36.1 us  [the longest x1 18.9 us: whole_video(): weights = lax.all_to_all(packed, 'row', 0, 0, tiled=True)]
    all_to_all x1 -> x0, starting transfers between devices: 5.33 us -> none  [whole_video(): weights = lax.all_to_all(packed, 'row', 0, 0, tiled=True)]
    ppermute x1, waiting for transfers between devices: 8.07 us -> 2.75 us  [everyone(): return (cells, lax.ppermute(cells, 'row', pairs), held)]
    ppermute x0 -> x3, starting transfers between devices: none -> 5.11 us  [the longest x1 4.25 us: everyone(): one = lax.ppermute(sent, ('grp', 'row'), to_one)]
    unnamed x20 -> x8, local copies, waits for them, and re-layouts: 3.44 us -> 0.02 us
    ppermute x3 -> x2, starting transfers between devices: 6.45 us -> 4.3 us  [everyone(): other = lax.ppermute(sent, 'row', pairs)]
    pallas_call x3 -> x4, Pallas kernels: 21.4 us -> 19.5 us  [the longest x1 10.7 us: whole_video(): middle(near, far, jnp.asarray(spread, bf16), w_in.reshape(3 * depth, chan...]
    ppermute x0 -> x3, waiting for transfers between devices: none -> 0.85 us  [the longest x1 0.84 us: everyone(): one = lax.ppermute(sent, ('grp', 'row'), to_one)]
  transfers between devices with their start and end apart: 5 -> 6, of which waited for: 3 -> 3; matrix products, arithmetic and copies ran while one was open for 1% -> 1% of each run, Pallas kernels for 24% -> 8%
where the time goes in v1:
time: 74.8 us; the launch traced here: 74.6 us
  blocking collectives  36.1 us (48%)
  Pallas kernels  21 us (28%)
  starting transfers between devices  11 us (15%)
  waiting for transfers between devices  5.64 us (8%)
  other arithmetic  0.78 us (1%)
    all_to_all x1, blocking collectives, whole_video(): weights = lax.all_to_all(packed, 'row', 0, 0, tiled=True)  18.9 us
    all_to_all x1, blocking collectives, whole_video(): swapped = lax.all_to_all(decoded, ('grp', 'row'), 0, 0, tiled=True)  17.1 us
    pallas_call x1, Pallas kernels, whole_video(): middle(near, far, jnp.asarray(spread, bf16), w_in.reshape(3 * depth, chan...  10.7 us
    ppermute x2, starting transfers between devices, everyone(): other = lax.ppermute(sent, 'row', pairs)  4.3 us
    ppermute x1, starting transfers between devices, everyone(): one = lax.ppermute(sent, ('grp', 'row'), to_one)  4.25 us
    pallas_call x1, Pallas kernels, whole_video(): near_out, fold_all, fold_new = first(weights, added, gain)  3.44 us
    ppermute x1, waiting for transfers between devices, everyone(): return (cells, lax.ppermute(cells, 'row', pairs), held)  2.75 us
    pallas_call x1, Pallas kernels, whole_video(): call(pack_kernel, shape((count, share, tiles * LANES), bf16), [pltpu.VMEM...  2.74 us
  transfers between devices with their start and end apart: 6, of which 3 were waited for; matrix products, arithmetic and copies ran while one was open for 1% of the time, Pallas kernels for 8%

profile of v1, /device:TPU:0, one launch (start us, length us, event | category | flops | bytes accessed | tf_op | source)
XLA Modules:
  0.0 74.6 jit_solution(17778498742916566268)
XLA Ops:
  0.0 0.0 copy-start.3
  0.0 0.0 copy-start.1
  0.0 0.0 copy-start
  0.0 0.8 %collective-permute-start.1 = (bf16[1,32,48]{2,1,0:T(8,128)(2,1)}, bf16[1,32,48]{2,1,0:T(8,128)(2,1)S(1)}, u32[]{:S(2)}, u32[]{:S(2)}) collective-permute-start(bf16[1,32,48]{2,1,0:T(8,128)(2,1)} %bitcast.12), channel_id=1, source_target_pairs={{1,16},{3,18},{5,20},{7,22},{9,24},{11,26},{13,28},{15,30},{16,1},... | collective-permute-start | bytes 9224 | tf_op jit(solution)/shard_map/ppermute | solution.py:632
  0.8 4.3 %collective-permute-start = (bf16[1,32,48]{2,1,0:T(8,128)(2,1)}, bf16[1,32,48]{2,1,0:T(8,128)(2,1)S(1)}, u32[]{:S(2)}, u32[]{:S(2)}) collective-permute-start(bf16[1,32,48]{2,1,0:T(8,128)(2,1)} %bitcast.13), channel_id=1, source_target_pairs={{0,16},{1,0},{2,18},{3,2},{4,20},{5,4},{6,22},{7,6},{8,24},{9,8},{... | collective-permute-start | bytes 9224 | tf_op jit(solution)/shard_map/ppermute | solution.py:631
  5.1 0.7 broadcast_select_fusion
  5.8 0.0 collective-permute-done.1
  5.8 0.8 %collective-permute-done = bf16[1,32,48]{2,1,0:T(8,128)(2,1)S(1)} collective-permute-done((bf16[1,32,48]{2,1,0:T(8,128)(2,1)}, bf16[1,32,48]{2,1,0:T(8,128)(2,1)S(1)}, u32[]{:S(2)}, u32[]{:S(2)}) %collective-permute-start) | collective-permute-done | bytes 3104 | tf_op jit(solution)/shard_map/ppermute | solution.py:631
  6.6 2.7 %collective-permute-start.2 = (bf16[2,32,48]{2,1,0:T(8,128)(2,1)S(1)}, bf16[2,32,48]{2,1,0:T(8,128)(2,1)S(1)}, u32[]{:S(2)}, u32[]{:S(2)}) collective-permute-start(bf16[2,32,48]{2,1,0:T(8,128)(2,1)S(1)} %pad_maximum_fusion.2), channel_id=1, source_target_pairs={{0,8},{1,9},{2,10},{3,11},{4,12},{5,13},{6,14},{7,15},{8,0},{9,1},... | collective-permute-start | bytes 18440 | tf_op jit(solution)/shard_map/ppermute | solution.py:641
  9.3 2.0 %collective-permute-done.2 = bf16[2,32,48]{2,1,0:T(8,128)(2,1)S(1)} collective-permute-done((bf16[2,32,48]{2,1,0:T(8,128)(2,1)S(1)}, bf16[2,32,48]{2,1,0:T(8,128)(2,1)S(1)}, u32[]{:S(2)}, u32[]{:S(2)}) %collective-permute-start.2) | collective-permute-done | bytes 6176 | tf_op jit(solution)/shard_map/ppermute | solution.py:641
  11.4 1.6 %collective-permute-start.3 = (bf16[4,32,48]{2,1,0:T(8,128)(2,1)S(1)}, bf16[4,32,48]{2,1,0:T(8,128)(2,1)S(1)}, u32[]{:S(2)}, u32[]{:S(2)}) collective-permute-start(bf16[4,32,48]{2,1,0:T(8,128)(2,1)S(1)} %pad_maximum_fusion.1), channel_id=1, source_target_pairs={{0,4},{1,5},{2,6},{3,7},{4,0},{5,1},{6,2},{7,3},{8,12},{9,13},{10,... | collective-permute-start | bytes 36872 | tf_op jit(solution)/shard_map/ppermute | solution.py:641
  13.0 2.7 %shard_map.100 = bf16[16,16,896]{2,1,0:T(8,128)(2,1)S(1)} custom-call(bf16[27,32,512]{2,1,0:T(8,128)(2,1)} %w_any.1), custom_call_target="tpu_custom_call" | custom-call | flops 1000000 | bytes 2000000 | tf_op jit(solution)/shard_map/pallas_call | solution.py:660
  15.8 0.0 collective-permute-done.3
  15.8 1.6 %collective-permute-start.4 = (bf16[8,32,48]{2,1,0:T(8,128)(2,1)S(1)}, bf16[8,32,48]{2,1,0:T(8,128)(2,1)S(1)}, u32[]{:S(2)}, u32[]{:S(2)}) collective-permute-start(bf16[8,32,48]{2,1,0:T(8,128)(2,1)S(1)} %pad_maximum_fusion.near_ref), channel_id=1, source_target_pairs={{0,2},{1,3},{2,0},{3,1},{4,6},{5,7},{6,4},{7,5},{8,10},{9,11},{10,... | collective-permute-start | bytes 73736 | tf_op jit(solution)/shard_map/ppermute | solution.py:640
  17.4 2.7 %collective-permute-done.4.far_ref = bf16[8,32,48]{2,1,0:T(8,128)(2,1)S(1)} collective-permute-done((bf16[8,32,48]{2,1,0:T(8,128)(2,1)S(1)}, bf16[8,32,48]{2,1,0:T(8,128)(2,1)S(1)}, u32[]{:S(2)}, u32[]{:S(2)}) %collective-permute-start.4) | collective-permute-done | bytes 24608 | tf_op jit(solution)/shard_map/ppermute | solution.py:640
  20.1 0.0 copy-done.3
  20.1 0.0 copy-done.1
  20.1 0.0 copy-done
  20.1 0.0 copy-start.2
  20.1 10.7 %shard_map.101.x_ref = bf16[1536,512]{1,0:T(8,128)(2,1)S(1)} custom-call(bf16[8,32,48]{2,1,0:T(8,128)(2,1)S(1)} %pad_maximum_fusion.near_ref, bf16[8,32,48]{2,1,0:T(8,128)(2,1)S(1)} %collective-permute-done.4.far_ref, bf16[128,144]{1,0:T(8,128)(2,1)S(1)} %copy-done.3, bf16[432,512]{1,0:T(8,128)(2,1)S(1)} %bitcast.8, f32[1,512]{1,0:T(1,128)S(1)} %bitcast.9, ...), custom_call_target="tpu_custom_call" | custom-call | flops 7000000000 | bytes 6000000 | tf_op jit(solution)/shard_map/pallas_call | solution.py:701
  30.8 0.1 collective-permute-start.5
  30.9 18.9 %all_to_all.10 = bf16[16,16,896]{2,1,0:T(8,128)(2,1)S(1)} all-to-all(bf16[16,16,896]{2,1,0:T(8,128)(2,1)S(1)} %shard_map.100), channel_id=1, replica_groups=mesh['grp'=2,'row'=16] {'row'}, dimensions={0} | all-to-all | bytes 917504 | tf_op jit(solution)/shard_map/all_to_all | solution.py:676
  49.8 0.0 copy-done.2
  49.8 3.4 %shard_map.102 = (bf16[16,48,128]{2,1,0:T(8,128)(2,1)S(1)}, bf16[512,512]{1,0:T(8,128)(2,1)S(1)}, bf16[512,512]{1,0:T(8,128)(2,1)S(1)}) custom-call(bf16[256,896]{1,0:T(8,128)(2,1)S(1)} %bitcast.7, bf16[1536,512]{1,0:T(8,128)(2,1)S(1)} %shard_map.101.x_ref, f32[1,512]{1,0:T(1,128)S(1)} %bitcast.10), custom_call_target="tpu_custom_call" | custom-call | flops 2000000000 | bytes 3000000 | tf_op jit(solution)/shard_map/pallas_call | solution.py:732
  53.3 0.0 collective-permute-done.5.x_ref
  53.3 2.7 %shard_map.103 = bf16[32,48,128]{2,1,0:T(8,128)(2,1)S(1)} custom-call(bf16[16,48,128]{2,1,0:T(8,128)(2,1)S(1)} %get-tuple-element.12.near_ref, bf16[1536,512]{1,0:T(8,128)(2,1)S(1)} %collective-permute-done.5.x_ref, bf16[512,512]{1,0:T(8,128)(2,1)S(1)} %get-tuple-element.13.all_ref, bf16[512,512]{1,0:T(8,128)(2,1)S(1)} %get-tuple-element.14.new_ref, ...), custom_call_target="tpu_custom_call" | custom-call | flops 2000000000 | bytes 3000000 | tf_op jit(solution)/shard_map/pallas_call | solution.py:734
  55.9 17.1 %all_to_all.11.x_ref = bf16[32,48,128]{2,1,0:T(8,128)(2,1)S(1)} all-to-all(bf16[32,48,128]{2,1,0:T(8,128)(2,1)S(1)} %shard_map.103), channel_id=1, replica_groups=mesh['grp'=2,'row'=16] {'grp','row'}, dimensions={0} | all-to-all | bytes 786432 | tf_op jit(solution)/shard_map/all_to_all | solution.py:743
  73.1 1.5 %shard_map.104 = bf16[2,2,96,512]{3,2,1,0:T(8,128)(2,1)} custom-call(bf16[32,48,128]{2,1,0:T(8,128)(2,1)S(1)} %all_to_all.11.x_ref), custom_call_target="tpu_custom_call" | custom-call | flops 1000000 | bytes 1000000 | tf_op jit(solution)/shard_map/pallas_call | solution.py:744
  (4 shorter events, 0.0 us)
Async XLA Ops:
  0.0 20.1 %copy-start.3 = (bf16[128,144]{1,0:T(8,128)(2,1)S(1)}, bf16[128,144]{1,0:T(8,128)(2,1)}, u32[]{:S(2)}) copy-start(bf16[128,144]{1,0:T(8,128)(2,1)} %constant.29.clone.spread_ref) | copy-start | bytes 110596
  0.0 20.1 %copy-start.1 = (f32[512]{0:T(512)S(1)}, f32[512]{0:T(512)}, u32[]{:S(2)}) copy-start(f32[512]{0:T(512)} %param.12) | copy-start | bytes 6148
  0.0 20.1 %copy-start = (bf16[27,16,512]{2,1,0:T(8,128)(2,1)S(1)}, bf16[27,16,512]{2,1,0:T(8,128)(2,1)}, u32[]{:S(2)}) copy-start(bf16[27,16,512]{2,1,0:T(8,128)(2,1)} %param.11) | copy-start | bytes 1327108
  0.0 5.8 %collective-permute-start.1 = (bf16[1,32,48]{2,1,0:T(8,128)(2,1)}, bf16[1,32,48]{2,1,0:T(8,128)(2,1)S(1)}, u32[]{:S(2)}, u32[]{:S(2)}) collective-permute-start(bf16[1,32,48]{2,1,0:T(8,128)(2,1)} %bitcast.12), channel_id=1, source_target_pairs={{1,16},{3,18},{5,20},{7,22},{9,24},{11,26},{13,28},{15,30},{16,1},... | collective-permute-start | bytes 9224 | tf_op jit(solution)/shard_map/ppermute | solution.py:632
  0.8 5.8 %collective-permute-start = (bf16[1,32,48]{2,1,0:T(8,128)(2,1)}, bf16[1,32,48]{2,1,0:T(8,128)(2,1)S(1)}, u32[]{:S(2)}, u32[]{:S(2)}) collective-permute-start(bf16[1,32,48]{2,1,0:T(8,128)(2,1)} %bitcast.13), channel_id=1, source_target_pairs={{0,16},{1,0},{2,18},{3,2},{4,20},{5,4},{6,22},{7,6},{8,24},{9,8},{... | collective-permute-start | bytes 9224 | tf_op jit(solution)/shard_map/ppermute | solution.py:631
  6.6 4.7 %collective-permute-start.2 = (bf16[2,32,48]{2,1,0:T(8,128)(2,1)S(1)}, bf16[2,32,48]{2,1,0:T(8,128)(2,1)S(1)}, u32[]{:S(2)}, u32[]{:S(2)}) collective-permute-start(bf16[2,32,48]{2,1,0:T(8,128)(2,1)S(1)} %pad_maximum_fusion.2), channel_id=1, source_target_pairs={{0,8},{1,9},{2,10},{3,11},{4,12},{5,13},{6,14},{7,15},{8,0},{9,1},... | collective-permute-start | bytes 18440 | tf_op jit(solution)/shard_map/ppermute | solution.py:641
  11.4 4.4 %collective-permute-start.3 = (bf16[4,32,48]{2,1,0:T(8,128)(2,1)S(1)}, bf16[4,32,48]{2,1,0:T(8,128)(2,1)S(1)}, u32[]{:S(2)}, u32[]{:S(2)}) collective-permute-start(bf16[4,32,48]{2,1,0:T(8,128)(2,1)S(1)} %pad_maximum_fusion.1), channel_id=1, source_target_pairs={{0,4},{1,5},{2,6},{3,7},{4,0},{5,1},{6,2},{7,3},{8,12},{9,13},{10,... | collective-permute-start | bytes 36872 | tf_op jit(solution)/shard_map/ppermute | solution.py:641
  15.8 4.3 %collective-permute-start.4 = (bf16[8,32,48]{2,1,0:T(8,128)(2,1)S(1)}, bf16[8,32,48]{2,1,0:T(8,128)(2,1)S(1)}, u32[]{:S(2)}, u32[]{:S(2)}) collective-permute-start(bf16[8,32,48]{2,1,0:T(8,128)(2,1)S(1)} %pad_maximum_fusion.near_ref), channel_id=1, source_target_pairs={{0,2},{1,3},{2,0},{3,1},{4,6},{5,7},{6,4},{7,5},{8,10},{9,11},{10,... | collective-permute-start | bytes 73736 | tf_op jit(solution)/shard_map/ppermute | solution.py:640
  20.1 29.7 %copy-start.2 = (f32[512]{0:T(512)S(1)}, f32[512]{0:T(512)}, u32[]{:S(2)}) copy-start(f32[512]{0:T(512)} %param.17) | copy-start | bytes 6148
  30.8 22.5 %collective-permute-start.5 = (bf16[1536,512]{1,0:T(8,128)(2,1)S(1)}, bf16[1536,512]{1,0:T(8,128)(2,1)S(1)}, u32[]{:S(2)}, u32[]{:S(2)}) collective-permute-start(bf16[1536,512]{1,0:T(8,128)(2,1)S(1)} %shard_map.101.x_ref), channel_id=1, source_target_pairs={{0,1},{1,0},{2,3},{3,2},{4,5},{5,4},{6,7},{7,6},{8,9},{9,8},{10,11... | collective-permute-start | bytes 4718600 | tf_op jit(solution)/shard_map/ppermute | solution.py:733

commit v2 on v1

--- a/solution.py
+++ b/solution.py
@@ -252,38 +252,31 @@
 
 
 def mid_kernel(
-    dims, near_ref, far_ref, spread_ref, w_in_ref, gain_ref, wq_any, wk_any, wv_any, wo_any, out_ref,
+    dims, z_ref, spread_ref, w_in_ref, gain_ref, wq_any, wk_any, wv_any, wo_any, out_ref,
     x32, wide, edge, h_ref, q_ref, k_ref, v_ref, wq_ref, wk_ref, wv_ref, wo_ref, sems,
 ):
     pairs = ((wq_any, wq_ref), (wk_any, wk_ref), (wv_any, wv_ref), (wo_any, wo_ref))
     loads = [pltpu.make_async_copy(a, b, sems.at[k]) for k, (a, b) in enumerate(pairs)]
     for load in loads:
         load.start()
-    frames, rows, own, cols, zc, chan, chunk = dims
+    frames, rows, _, cols, zc, chan, chunk = dims
     per_frame = rows * cols
     total = frames * per_frame
     step = per_frame // 2
     per_tile = LANES // zc
     block = lane_iota(LANES) // zc
-    me = lax.axis_index("row")
-    order = rounds(rows // own)
-
-    def piece(row, at):
-        differs = me ^ (row // own)
-        place = sum(
-            ((differs >> (bit.bit_length() - 1)) & 1) << r for r, bit in enumerate(order[:-1])
-        )
-        return jnp.where(differs & order[-1] == 0, near_ref[place, at, :], far_ref[place, at, :])
-
-    for f in range(frames):
-        for g in range(rows // per_tile):
-            tile = jnp.concatenate(
-                [piece(g * per_tile + i, slice(f * zc, (f + 1) * zc)) for i in range(per_tile)], 0
-            ).astype(jnp.float32)
-            turned = tile.T
+    first_row = lax.axis_index("row") % 2 * rows
+    half = LANES // frames
+    for g in range(rows // per_tile):
+        tile = jnp.concatenate(
+            [z_ref[first_row + g * per_tile + i] for i in range(per_tile)], 0
+        ).astype(jnp.float32)
+        turned = tile.T
+        for f in range(frames):
+            field = turned[f * half : f * half + cols]
             for i in range(per_tile):
                 at = f * per_frame + (g * per_tile + i) * cols
-                x32[at : at + cols, :] = jnp.where(block == i, turned, 0.0).astype(x32.dtype)
+                x32[at : at + cols, :] = jnp.where(block == i, field, 0.0).astype(x32.dtype)
 
     lane = lane_iota(edge.shape[2])
     col_tap = (lane // zc) % 3
@@ -442,14 +435,34 @@
                 to_ref[at : at + share, :] = v[k * share : (k + 1) * share]
 
 
-def up_video(dims, x_ref, all_ref, new_ref, gain_ref, t_ref, m0_ref, m2_ref, store):
+def over_blocks(row, share):
+    step = share
+    while step < LANES:
+        row = row + pltpu.roll(row, step, 1)
+        step *= 2
+    return row
+
+
+def gain_kernel(share, gain_ref, out_ref):
+    chan = gain_ref.shape[1]
+    me = lax.axis_index("grp") * lax.axis_size("row") + lax.axis_index("row")
+    gains = jnp.broadcast_to(gain_ref[...], (8, chan))
+    gains = jnp.where(lane_iota(chan) // share == me, gains, 0.0)
+    gains = sum(gains[:, k : k + LANES] for k in range(0, chan, LANES))
+    out_ref[...] = over_blocks(gains, share)
+
+
+def up_video(dims, ready, x_ref, all_ref, new_ref, gain_ref, t_ref, m0_ref, m2_ref, store):
     rows, cols, chan, share, _ = dims
     per_frame = rows * cols
     width = LANES
 
+    ready(0)
     t_ref[...] = jnp.dot(
         x_ref[0:per_frame, :], all_ref[...], preferred_element_type=jnp.float32
-    ) + jnp.dot(
+    )
+    ready(1)
+    t_ref[...] += jnp.dot(
         x_ref[per_frame : 2 * per_frame, :], new_ref[...], preferred_element_type=jnp.float32
     )
     lane = lane_iota(width)
@@ -489,15 +502,8 @@
     group = chan // GROUPS
     count = 2 * rows * cols * 4 * group
 
-    def over_blocks(row):
-        step = share
-        while step < width:
-            row = row + pltpu.roll(row, step, 1)
-            step *= 2
-        return row
-
     def grouped(part):
-        return group_sum(over_blocks(all_rows(part)), group)
+        return group_sum(over_blocks(all_rows(part), share), group)
 
     mean_row = (grouped(part) / count)[0:1]
 
@@ -507,11 +513,7 @@
 
     part = lax.fori_loop(0, rows, spreadness, jnp.zeros((8, width), jnp.float32), unroll=2)
     variance = grouped(part) / count
-    me = lax.axis_index("grp") * lax.axis_size("row") + lax.axis_index("row")
-    gains = jnp.broadcast_to(gain_ref[...], (8, chan))
-    gains = jnp.where(lane_iota(chan) // share == me, gains, 0.0)
-    gains = over_blocks(sum(gains[:, k : k + width] for k in range(0, chan, width)))
-    scale_row = (lax.rsqrt(variance + norm_eps) * gains)[0:1]
+    scale_row = (lax.rsqrt(variance + norm_eps) * gain_ref[...])[0:1]
 
     def finish(d, _):
         at = pl.ds(pl.multiple_of(d * cols, 8), cols)
@@ -530,13 +532,21 @@
     def store(d, v):
         out_ref[d] = v.astype(out_ref.dtype)
 
-    up_video(dims, x_ref, all_ref, new_ref, gain_ref, t_ref, m0_ref, m2_ref, store)
+    def ready(f):
+        pass
+
+    up_video(dims, ready, x_ref, all_ref, new_ref, gain_ref, t_ref, m0_ref, m2_ref, store)
 
 
 def far_kernel(
-    dims, near_ref, x_ref, all_ref, new_ref, gain_ref, out_ref, t_ref, m0_ref, m2_ref
+    dims, near_ref, x_any, all_ref, new_ref, gain_ref, out_ref, t_ref, m0_ref, m2_ref, x_ref, sems
 ):
-    rows = dims[0]
+    rows, cols = dims[:2]
+    loads = []
+    for f in range(2):
+        at = slice(f * rows * cols, (f + 1) * rows * cols)
+        loads.append(pltpu.make_async_copy(x_any.at[at], x_ref.at[at], sems.at[f]))
+        loads[-1].start()
     video = lax.axis_index("row") % 2
 
     def keep(d, _):
@@ -548,7 +558,10 @@
     def store(d, v):
         out_ref[(1 - video) * rows + d] = v.astype(out_ref.dtype)
 
-    up_video(dims, x_ref, all_ref, new_ref, gain_ref, t_ref, m0_ref, m2_ref, store)
+    def ready(f):
+        loads[f].wait()
+
+    up_video(dims, ready, x_ref, all_ref, new_ref, gain_ref, t_ref, m0_ref, m2_ref, store)
 
 
 def place_kernel(share, x_ref, out_ref, line):
@@ -586,7 +599,7 @@
         and chan == GROUPS * share
         and zc == 16
         and cols % 16 == 0
-        and cols <= LANES
+        and cols <= LANES // frames
         and (rows * cols) % 256 == 0
         and rows * cols <= 1024
     )
@@ -602,44 +615,6 @@
         compiler_params=pltpu.CompilerParams(vmem_limit_bytes=limit * MIB),
         cost_estimate=pl.CostEstimate(flops=flops, bytes_accessed=moved, transcendentals=0),
     )
-
-
-def rounds(count):
-    bits = [1]
-    bit = count // 2
-    while bit > 1:
-        bits.append(bit)
-        bit //= 2
-    return bits
-
-
-def everyone(cells, held):
-    count = lax.axis_size("row")
-    me = lax.axis_index("row")
-    grp = lax.axis_index("grp")
-    sent = cells[None]
-    own = lax.optimization_barrier(jnp.where(me < count, sent, 0))
-    to_one, to_two = [], []
-    for g in range(2):
-        for k in range(count):
-            here = g * count + k
-            if g == k % 2:
-                to_one.append((here, (1 - g) * count + k))
-            else:
-                to_one.append((here, g * count + (k ^ 1)))
-                to_two.append((here, (1 - g) * count + (k ^ 1)))
-    one = lax.ppermute(sent, ("grp", "row"), to_one)
-    two = lax.ppermute(sent, ("grp", "row"), to_two)
-    mine = grp == me % 2
-    cells = sent = jnp.concatenate([jnp.where(mine, own, one), jnp.where(mine, one, two)], 0)
-    order = rounds(count)
-    for bit in order[1:]:
-        pairs = [(k, k ^ bit) for k in range(count)]
-        if bit == order[-1]:
-            cells, held = lax.optimization_barrier((cells, held))
-            return cells, lax.ppermute(cells, "row", pairs), held
-        other = lax.ppermute(sent, "row", pairs)
-        cells = sent = jnp.concatenate([cells, other], 0)
 
 
 def whole_video(latent, w_in, gain_in, w_query, w_key, w_value, w_out, gain_up, w_up):
@@ -655,9 +630,14 @@
     shape = jax.ShapeDtypeStruct
     chunk = 256
 
-    cells = jnp.swapaxes(latent, 2, 3).reshape(frames * zc, cols)
-
-    packed = call(
+    half = LANES // frames
+    cells = jnp.swapaxes(latent.reshape(frames, cols, zc), 1, 2)
+    cells = jnp.pad(cells, ((0, 0), (0, 0), (0, half - cols)))
+    cells = jnp.concatenate([cells[f] for f in range(frames)], 1)
+    cells = jnp.broadcast_to(cells, (2 * count, zc, LANES))
+    cells = lax.all_to_all(cells, ("grp", "row"), 0, 0, tiled=True)
+
+    pack = call(
         pack_kernel,
         shape((count, share, tiles * LANES), bf16),
         [
@@ -671,8 +651,8 @@
         2 * 10**6,
         (pltpu.HBM,),
         pltpu.HBM,
-    )(pltpu.with_memory_space_constraint(w_up, pltpu.HBM))
-    near, far, packed = everyone(cells, packed)
+    )
+    packed = pack(pltpu.with_memory_space_constraint(w_up, pltpu.HBM))
     weights = lax.all_to_all(packed, "row", 0, 0, tiled=True)
     weights = weights.reshape(chan // 2, tiles * LANES)
 
@@ -696,11 +676,10 @@
         28,
         7 * 10**9,
         6 * 10**6,
-        (pltpu.VMEM,) * 5 + (pltpu.HBM,) * 4,
+        (pltpu.VMEM,) * 4 + (pltpu.HBM,) * 4,
     )
     added = middle(
-        near,
-        far,
+        cells,
         jnp.asarray(spread, bf16),
         w_in.reshape(3 * depth, chan),
         gain_in.reshape(1, chan),
@@ -712,7 +691,11 @@
 
     dims = (rows, cols, chan, share, chunk)
     width = 4 * LANES
-    gain = gain_up.reshape(1, chan)
+    gains = call(
+        functools.partial(gain_kernel, share), shape((8, LANES), f32), [], 1, 10**4, 10**4,
+        (pltpu.VMEM,),
+    )
+    gain = gains(gain_up.reshape(1, chan))
     fields = [
         pltpu.VMEM((rows * cols, width), f32),
         pltpu.VMEM((rows * cols, LANES), f32),
@@ -734,12 +717,12 @@
     decoded = call(
         functools.partial(far_kernel, dims),
         shape((2 * count, cols, LANES), bf16),
-        fields,
+        fields + [pltpu.VMEM(added.shape, bf16), pltpu.SemaphoreType.DMA((2,))],
         16,
         2 * 10**9,
         3 * 10**6,
-        (pltpu.VMEM,) * 5,
-    )(near_out, other, fold_all, fold_new, gain)
+        (pltpu.VMEM, pltpu.HBM) + (pltpu.VMEM,) * 3,
+    )(near_out, pltpu.with_memory_space_constraint(other, pltpu.HBM), fold_all, fold_new, gain)
     swapped = lax.all_to_all(decoded, ("grp", "row"), 0, 0, tiled=True)
     return call(
         functools.partial(place_kernel, share),

time: 74.8 us -> 73.7 us (0.985)
  waiting for transfers between devices: 5.64 us -> 13 us
  starting transfers between devices: 11 us -> 3.9 us
  blocking collectives: 36.1 us -> 30.9 us
  local copies, waits for them, and re-layouts: 0.02 us -> 3.27 us
  Pallas kernels: 21 us -> 22.1 us
    all_to_all x0 -> x1, waiting for transfers between devices: none -> 13 us  [whole_video(): weights = lax.all_to_all(packed, 'row', 0, 0, tiled=True)]
    ppermute x5 -> x0, starting transfers between devices: 10.9 us -> none  [the longest x2 4.3 us: everyone(): other = lax.ppermute(sent, 'row', pairs)]
    ppermute x5 -> x0, waiting for transfers between devices: 5.64 us -> none  [the longest x1 2.75 us: everyone(): return (cells, lax.ppermute(cells, 'row', pairs), held)]
    all_to_all x1, blocking collectives: 18.9 us -> 15.3 us  [whole_video(): cells = lax.all_to_all(cells, ('grp', 'row'), 0, 0, tiled=True)]
    all_to_all x0 -> x1, starting transfers between devices: none -> 3.57 us  [whole_video(): weights = lax.all_to_all(packed, 'row', 0, 0, tiled=True)]
    unnamed x8, local copies, waits for them, and re-layouts: 0.02 us -> 2.54 us
    all_to_all x1, blocking collectives: 17.1 us -> 15.6 us  [whole_video(): swapped = lax.all_to_all(decoded, ('grp', 'row'), 0, 0, tiled=True)]
    pallas_call x1, Pallas kernels: 2.65 us -> 3.82 us  [whole_video(): call(functools.partial(far_kernel, dims), shape((2 * count, cols, LANES),...]
  transfers between devices with their start and end apart: 6 -> 2, of which waited for: 3 -> 1; matrix products, arithmetic and copies ran while one was open for 1% -> 0% of each run, Pallas kernels for 8% -> 8%
where the time goes in v2:
time: 73.7 us; the launch traced here: 73.3 us
  blocking collectives  30.9 us (42%)
  Pallas kernels  22.1 us (30%)
  waiting for transfers between devices  13 us (18%)
  starting transfers between devices  3.9 us (5%)
  local copies, waits for them, and re-layouts  3.27 us (4%)
    all_to_all x1, blocking collectives, whole_video(): swapped = lax.all_to_all(decoded, ('grp', 'row'), 0, 0, tiled=True)  15.6 us
    all_to_all x1, blocking collectives, whole_video(): cells = lax.all_to_all(cells, ('grp', 'row'), 0, 0, tiled=True)  15.3 us
    all_to_all x1, waiting for transfers between devices, whole_video(): weights = lax.all_to_all(packed, 'row', 0, 0, tiled=True)  13 us
    pallas_call x1, Pallas kernels, whole_video(): middle(cells, jnp.asarray(spread, bf16), w_in.reshape(3 * depth, chan), g...  10.6 us
    pallas_call x1, Pallas kernels, whole_video(): call(functools.partial(far_kernel, dims), shape((2 * count, cols, LANES),...  3.82 us
    all_to_all x1, starting transfers between devices, whole_video(): weights = lax.all_to_all(packed, 'row', 0, 0, tiled=True)  3.57 us
    pallas_call x1, Pallas kernels, whole_video(): near_out, fold_all, fold_new = first(weights, added, gain)  3.34 us
    pallas_call x1, Pallas kernels, whole_video(): packed = pack(pltpu.with_memory_space_constraint(w_up, pltpu.HBM))  2.62 us
  transfers between devices with their start and end apart: 2, of which 1 were waited for; matrix products, arithmetic and copies ran while one was open for 0% of the time, Pallas kernels for 8%

profile of v2, /device:TPU:0, one launch (start us, length us, event | category | flops | bytes accessed | tf_op | source)
XLA Modules:
  0.0 73.3 jit_solution(12961959744857497601)
XLA Ops:
  0.0 0.7 fusion
  0.7 0.1 pad_maximum_fusion
  0.8 15.3 %all_to_all.15.z_ref = bf16[32,16,128]{2,1,0:T(8,128)(2,1)S(1)} all-to-all(bf16[32,16,128]{2,1,0:T(8,128)(2,1)S(1)} %broadcast_in_dim.3), channel_id=1, replica_groups=mesh['grp'=2,'row'=16] {'grp','row'}, dimensions={0} | all-to-all | bytes 262144 | tf_op jit(solution)/shard_map/all_to_all | solution.py:638
  16.2 0.0 copy-start.1
  16.2 1.0 %copy-done.1 = bf16[27,16,512]{2,1,0:T(8,128)(2,1)S(1)} copy-done((bf16[27,16,512]{2,1,0:T(8,128)(2,1)S(1)}, bf16[27,16,512]{2,1,0:T(8,128)(2,1)}, u32[]{:S(2)}) %copy-start.1) | copy-done | bytes 442392
  17.2 0.0 copy-start.2
  17.2 0.7 copy-done.2
  17.8 0.0 copy-start.3
  17.8 0.8 %copy-done.3 = bf16[128,144]{1,0:T(8,128)(2,1)S(1)} copy-done((bf16[128,144]{1,0:T(8,128)(2,1)S(1)}, bf16[128,144]{1,0:T(8,128)(2,1)}, u32[]{:S(2)}) %copy-start.3) | copy-done | bytes 36888
  18.7 10.6 %shard_map.101.x_ref = bf16[1536,512]{1,0:T(8,128)(2,1)S(1)} custom-call(bf16[32,16,128]{2,1,0:T(8,128)(2,1)S(1)} %all_to_all.15.z_ref, bf16[128,144]{1,0:T(8,128)(2,1)S(1)} %copy-done.3, bf16[432,512]{1,0:T(8,128)(2,1)S(1)} %bitcast.13, f32[1,512]{1,0:T(1,128)S(1)} %bitcast.14, bf16[512,512]{1,0:T(8,128)(2,1)} %wq_any.1, bf16[512,512]{1,0:T(8,128)(2,1)} %wk_any.1, ...), custom_call_target="tpu_custom_call" | custom-call | flops 7000000000 | bytes 6000000 | tf_op jit(solution)/shard_map/pallas_call | solution.py:681
  29.3 0.0 copy-start
  29.3 0.3 collective-permute-start
  29.6 2.6 %shard_map.100 = bf16[16,16,896]{2,1,0:T(8,128)(2,1)} custom-call(bf16[27,32,512]{2,1,0:T(8,128)(2,1)} %w_any.1), custom_call_target="tpu_custom_call" | custom-call | flops 1000000 | bytes 2000000 | tf_op jit(solution)/shard_map/pallas_call | solution.py:655
  32.3 3.6 %all-to-all-start = ((bf16[16,16,896]{2,1,0:T(8,128)(2,1)}), bf16[16,16,896]{2,1,0:T(8,128)(2,1)S(1)}, u32[]{:S(2)}, u32[]{:S(2)}) async-start(bf16[16,16,896]{2,1,0:T(8,128)(2,1)} %shard_map.100), calls=%async_computation | async-start | bytes 917504 | tf_op jit(solution)/shard_map/all_to_all | solution.py:656
  35.9 0.0 copy-done
  35.9 0.2 shard_map.102.gain_ref
  36.1 13.0 %all-to-all-done = bf16[16,16,896]{2,1,0:T(8,128)(2,1)S(1)} async-done(((bf16[16,16,896]{2,1,0:T(8,128)(2,1)}), bf16[16,16,896]{2,1,0:T(8,128)(2,1)S(1)}, u32[]{:S(2)}, u32[]{:S(2)}) %all-to-all-start) | async-done | bytes 458784 | tf_op jit(solution)/shard_map/all_to_all | solution.py:656
  49.0 3.3 %shard_map.103 = (bf16[16,48,128]{2,1,0:T(8,128)(2,1)S(1)}, bf16[512,512]{1,0:T(8,128)(2,1)S(1)}, bf16[512,512]{1,0:T(8,128)(2,1)S(1)}) custom-call(bf16[256,896]{1,0:T(8,128)(2,1)S(1)} %bitcast.11, bf16[1536,512]{1,0:T(8,128)(2,1)S(1)} %shard_map.101.x_ref, f32[8,128]{1,0:T(8,128)S(1)} %shard_map.102.gain_ref), custom_call_target="tpu_custom_call" | custom-call | flops 2000000000 | bytes 3000000 | tf_op jit(solution)/shard_map/pallas_call | solution.py:715
  52.4 0.0 collective-permute-done.x_any
  52.4 3.8 %shard_map.104 = bf16[32,48,128]{2,1,0:T(8,128)(2,1)S(1)} custom-call(bf16[16,48,128]{2,1,0:T(8,128)(2,1)S(1)} %get-tuple-element.8.near_ref, bf16[1536,512]{1,0:T(8,128)(2,1)} %collective-permute-done.x_any, bf16[512,512]{1,0:T(8,128)(2,1)S(1)} %get-tuple-element.9.all_ref, bf16[512,512]{1,0:T(8,128)(2,1)S(1)} %get-tuple-element.10.new_ref, ...), custom_call_target="tpu_custom_call" | custom-call | flops 2000000000 | bytes 3000000 | tf_op jit(solution)/shard_map/pallas_call | solution.py:717
  56.2 15.6 %all_to_all.16.x_ref = bf16[32,48,128]{2,1,0:T(8,128)(2,1)S(1)} all-to-all(bf16[32,48,128]{2,1,0:T(8,128)(2,1)S(1)} %shard_map.104), channel_id=1, replica_groups=mesh['grp'=2,'row'=16] {'grp','row'}, dimensions={0} | all-to-all | bytes 786432 | tf_op jit(solution)/shard_map/all_to_all | solution.py:726
  71.8 1.5 %shard_map.105 = bf16[2,2,96,512]{3,2,1,0:T(8,128)(2,1)} custom-call(bf16[32,48,128]{2,1,0:T(8,128)(2,1)S(1)} %all_to_all.16.x_ref), custom_call_target="tpu_custom_call" | custom-call | flops 1000000 | bytes 1000000 | tf_op jit(solution)/shard_map/pallas_call | solution.py:727
  (1 shorter events, 0.0 us)
Async XLA Ops:
  16.2 1.0 %copy-start.1 = (bf16[27,16,512]{2,1,0:T(8,128)(2,1)S(1)}, bf16[27,16,512]{2,1,0:T(8,128)(2,1)}, u32[]{:S(2)}) copy-start(bf16[27,16,512]{2,1,0:T(8,128)(2,1)} %param.11) | copy-start | bytes 1327108
  17.2 0.7 copy-start.2
  17.8 0.8 %copy-start.3 = (bf16[128,144]{1,0:T(8,128)(2,1)S(1)}, bf16[128,144]{1,0:T(8,128)(2,1)}, u32[]{:S(2)}) copy-start(bf16[128,144]{1,0:T(8,128)(2,1)} %constant.5.clone.spread_ref) | copy-start | bytes 110596
  29.3 6.6 %copy-start = (f32[512]{0:T(512)S(1)}, f32[512]{0:T(512)}, u32[]{:S(2)}) copy-start(f32[512]{0:T(512)} %param.17) | copy-start | bytes 6148
  29.3 23.1 %collective-permute-start = (bf16[1536,512]{1,0:T(8,128)(2,1)S(1)}, bf16[1536,512]{1,0:T(8,128)(2,1)}, u32[]{:S(2)}, u32[]{:S(2)}) collective-permute-start(bf16[1536,512]{1,0:T(8,128)(2,1)S(1)} %shard_map.101.x_ref), channel_id=1, source_target_pairs={{0,1},{1,0},{2,3},{3,2},{4,5},{5,4},{6,7},{7,6},{8,9},{9,8},{10,11... | collective-permute-start | bytes 4718600 | tf_op jit(solution)/shard_map/ppermute | solution.py:716
  32.3 16.8 %all-to-all-start = ((bf16[16,16,896]{2,1,0:T(8,128)(2,1)}), bf16[16,16,896]{2,1,0:T(8,128)(2,1)S(1)}, u32[]{:S(2)}, u32[]{:S(2)}) async-start(bf16[16,16,896]{2,1,0:T(8,128)(2,1)} %shard_map.100), calls=%async_computation | async-start | bytes 917504 | tf_op jit(solution)/shard_map/all_to_all | solution.py:656

commit v3 on v2

--- a/solution.py
+++ b/solution.py
@@ -487,7 +487,7 @@
         ] + beside(t_ref[at, 3 * width : 4 * width])
         return 0
 
-    lax.fori_loop(0, rows, columns, 0, unroll=2)
+    lax.fori_loop(0, rows, columns, 0, unroll=rows)
 
     def lines(i, part):
         at = pl.ds(pl.multiple_of(i * cols, 8), cols)
@@ -498,7 +498,7 @@
         m0_ref[at, :] = v
         return part + fold_rows(v)
 
-    part = lax.fori_loop(0, rows, lines, jnp.zeros((8, width), jnp.float32), unroll=2)
+    part = lax.fori_loop(0, rows, lines, jnp.zeros((8, width), jnp.float32), unroll=rows)
     group = chan // GROUPS
     count = 2 * rows * cols * 4 * group
 
@@ -511,7 +511,7 @@
         v = m0_ref[pl.ds(pl.multiple_of(i * cols, 8), cols), :] - mean_row
         return part + fold_rows(v * v)
 
-    part = lax.fori_loop(0, rows, spreadness, jnp.zeros((8, width), jnp.float32), unroll=2)
+    part = lax.fori_loop(0, rows, spreadness, jnp.zeros((8, width), jnp.float32), unroll=rows)
     variance = grouped(part) / count
     scale_row = (lax.rsqrt(variance + norm_eps) * gain_ref[...])[0:1]
 
@@ -521,7 +521,7 @@
         store(d, v / (1.0 + jnp.exp(-v)))
         return 0
 
-    lax.fori_loop(0, rows, finish, 0, unroll=2)
+    lax.fori_loop(0, rows, finish, 0, unroll=rows)
 
 
 def near_kernel(

time: 73.7 us -> 72.8 us (0.988)
  Pallas kernels: 22.1 us -> 21.2 us
where the time goes in v3:
time: 72.8 us; the launch traced here: 72.4 us
  blocking collectives  30.9 us (42%)
  Pallas kernels  21.2 us (29%)
  waiting for transfers between devices  13 us (18%)
  starting transfers between devices  3.9 us (5%)
  local copies, waits for them, and re-layouts  3.27 us (4%)
    all_to_all x1, blocking collectives, whole_video(): swapped = lax.all_to_all(decoded, ('grp', 'row'), 0, 0, tiled=True)  15.6 us
    all_to_all x1, blocking collectives, whole_video(): cells = lax.all_to_all(cells, ('grp', 'row'), 0, 0, tiled=True)  15.3 us
    all_to_all x1, waiting for transfers between devices, whole_video(): weights = lax.all_to_all(packed, 'row', 0, 0, tiled=True)  13 us
    pallas_call x1, Pallas kernels, whole_video(): middle(cells, jnp.asarray(spread, bf16), w_in.reshape(3 * depth, chan), g...  10.6 us
    all_to_all x1, starting transfers between devices, whole_video(): weights = lax.all_to_all(packed, 'row', 0, 0, tiled=True)  3.57 us
    pallas_call x1, Pallas kernels, whole_video(): call(functools.partial(far_kernel, dims), shape((2 * count, cols, LANES),...  3.38 us
    pallas_call x1, Pallas kernels, whole_video(): near_out, fold_all, fold_new = first(weights, added, gain)  2.86 us
    pallas_call x1, Pallas kernels, whole_video(): packed = pack(pltpu.with_memory_space_constraint(w_up, pltpu.HBM))  2.62 us
  transfers between devices with their start and end apart: 2, of which 1 were waited for; matrix products, arithmetic and copies ran while one was open for 0% of the time, Pallas kernels for 8%

profile of v3, /device:TPU:0, one launch (start us, length us, event | category | flops | bytes accessed | tf_op | source)
XLA Modules:
  0.0 72.4 jit_solution(16127169963212147378)
XLA Ops:
  0.0 0.7 fusion
  0.7 0.1 pad_maximum_fusion
  0.8 15.3 %all_to_all.15.z_ref = bf16[32,16,128]{2,1,0:T(8,128)(2,1)S(1)} all-to-all(bf16[32,16,128]{2,1,0:T(8,128)(2,1)S(1)} %broadcast_in_dim.3), channel_id=1, replica_groups=mesh['grp'=2,'row'=16] {'grp','row'}, dimensions={0} | all-to-all | bytes 262144 | tf_op jit(solution)/shard_map/all_to_all | solution.py:638
  16.2 0.0 copy-start.1
  16.2 1.0 %copy-done.1 = bf16[27,16,512]{2,1,0:T(8,128)(2,1)S(1)} copy-done((bf16[27,16,512]{2,1,0:T(8,128)(2,1)S(1)}, bf16[27,16,512]{2,1,0:T(8,128)(2,1)}, u32[]{:S(2)}) %copy-start.1) | copy-done | bytes 442392
  17.2 0.0 copy-start.2
  17.2 0.7 copy-done.2
  17.8 0.0 copy-start.3
  17.8 0.8 %copy-done.3 = bf16[128,144]{1,0:T(8,128)(2,1)S(1)} copy-done((bf16[128,144]{1,0:T(8,128)(2,1)S(1)}, bf16[128,144]{1,0:T(8,128)(2,1)}, u32[]{:S(2)}) %copy-start.3) | copy-done | bytes 36888
  18.7 10.6 %shard_map.101.x_ref = bf16[1536,512]{1,0:T(8,128)(2,1)S(1)} custom-call(bf16[32,16,128]{2,1,0:T(8,128)(2,1)S(1)} %all_to_all.15.z_ref, bf16[128,144]{1,0:T(8,128)(2,1)S(1)} %copy-done.3, bf16[432,512]{1,0:T(8,128)(2,1)S(1)} %bitcast.13, f32[1,512]{1,0:T(1,128)S(1)} %bitcast.14, bf16[512,512]{1,0:T(8,128)(2,1)} %wq_any.1, bf16[512,512]{1,0:T(8,128)(2,1)} %wk_any.1, ...), custom_call_target="tpu_custom_call" | custom-call | flops 7000000000 | bytes 6000000 | tf_op jit(solution)/shard_map/pallas_call | solution.py:681
  29.3 0.0 copy-start
  29.3 0.3 collective-permute-start
  29.6 2.6 %shard_map.100 = bf16[16,16,896]{2,1,0:T(8,128)(2,1)} custom-call(bf16[27,32,512]{2,1,0:T(8,128)(2,1)} %w_any.1), custom_call_target="tpu_custom_call" | custom-call | flops 1000000 | bytes 2000000 | tf_op jit(solution)/shard_map/pallas_call | solution.py:655
  32.3 3.6 %all-to-all-start = ((bf16[16,16,896]{2,1,0:T(8,128)(2,1)}), bf16[16,16,896]{2,1,0:T(8,128)(2,1)S(1)}, u32[]{:S(2)}, u32[]{:S(2)}) async-start(bf16[16,16,896]{2,1,0:T(8,128)(2,1)} %shard_map.100), calls=%async_computation | async-start | bytes 917504 | tf_op jit(solution)/shard_map/all_to_all | solution.py:656
  35.9 0.0 copy-done
  35.9 0.2 shard_map.102.gain_ref
  36.1 13.0 %all-to-all-done = bf16[16,16,896]{2,1,0:T(8,128)(2,1)S(1)} async-done(((bf16[16,16,896]{2,1,0:T(8,128)(2,1)}), bf16[16,16,896]{2,1,0:T(8,128)(2,1)S(1)}, u32[]{:S(2)}, u32[]{:S(2)}) %all-to-all-start) | async-done | bytes 458784 | tf_op jit(solution)/shard_map/all_to_all | solution.py:656
  49.0 2.9 %shard_map.103 = (bf16[16,48,128]{2,1,0:T(8,128)(2,1)S(1)}, bf16[512,512]{1,0:T(8,128)(2,1)S(1)}, bf16[512,512]{1,0:T(8,128)(2,1)S(1)}) custom-call(bf16[256,896]{1,0:T(8,128)(2,1)S(1)} %bitcast.11, bf16[1536,512]{1,0:T(8,128)(2,1)S(1)} %shard_map.101.x_ref, f32[8,128]{1,0:T(8,128)S(1)} %shard_map.102.gain_ref), custom_call_target="tpu_custom_call" | custom-call | flops 2000000000 | bytes 3000000 | tf_op jit(solution)/shard_map/pallas_call | solution.py:715
  51.9 0.0 collective-permute-done.x_any
  51.9 3.4 %shard_map.104 = bf16[32,48,128]{2,1,0:T(8,128)(2,1)S(1)} custom-call(bf16[16,48,128]{2,1,0:T(8,128)(2,1)S(1)} %get-tuple-element.8.near_ref, bf16[1536,512]{1,0:T(8,128)(2,1)} %collective-permute-done.x_any, bf16[512,512]{1,0:T(8,128)(2,1)S(1)} %get-tuple-element.9.all_ref, bf16[512,512]{1,0:T(8,128)(2,1)S(1)} %get-tuple-element.10.new_ref, ...), custom_call_target="tpu_custom_call" | custom-call | flops 2000000000 | bytes 3000000 | tf_op jit(solution)/shard_map/pallas_call | solution.py:717
  55.3 15.6 %all_to_all.16.x_ref = bf16[32,48,128]{2,1,0:T(8,128)(2,1)S(1)} all-to-all(bf16[32,48,128]{2,1,0:T(8,128)(2,1)S(1)} %shard_map.104), channel_id=1, replica_groups=mesh['grp'=2,'row'=16] {'grp','row'}, dimensions={0} | all-to-all | bytes 786432 | tf_op jit(solution)/shard_map/all_to_all | solution.py:726
  70.9 1.5 %shard_map.105 = bf16[2,2,96,512]{3,2,1,0:T(8,128)(2,1)} custom-call(bf16[32,48,128]{2,1,0:T(8,128)(2,1)S(1)} %all_to_all.16.x_ref), custom_call_target="tpu_custom_call" | custom-call | flops 1000000 | bytes 1000000 | tf_op jit(solution)/shard_map/pallas_call | solution.py:727
  (1 shorter events, 0.0 us)
Async XLA Ops:
  16.2 1.0 %copy-start.1 = (bf16[27,16,512]{2,1,0:T(8,128)(2,1)S(1)}, bf16[27,16,512]{2,1,0:T(8,128)(2,1)}, u32[]{:S(2)}) copy-start(bf16[27,16,512]{2,1,0:T(8,128)(2,1)} %param.11) | copy-start | bytes 1327108
  17.2 0.7 copy-start.2
  17.8 0.8 %copy-start.3 = (bf16[128,144]{1,0:T(8,128)(2,1)S(1)}, bf16[128,144]{1,0:T(8,128)(2,1)}, u32[]{:S(2)}) copy-start(bf16[128,144]{1,0:T(8,128)(2,1)} %constant.5.clone.spread_ref) | copy-start | bytes 110596
  29.3 6.6 %copy-start = (f32[512]{0:T(512)S(1)}, f32[512]{0:T(512)}, u32[]{:S(2)}) copy-start(f32[512]{0:T(512)} %param.17) | copy-start | bytes 6148
  29.3 22.6 %collective-permute-start = (bf16[1536,512]{1,0:T(8,128)(2,1)S(1)}, bf16[1536,512]{1,0:T(8,128)(2,1)}, u32[]{:S(2)}, u32[]{:S(2)}) collective-permute-start(bf16[1536,512]{1,0:T(8,128)(2,1)S(1)} %shard_map.101.x_ref), channel_id=1, source_target_pairs={{0,1},{1,0},{2,3},{3,2},{4,5},{5,4},{6,7},{7,6},{8,9},{9,8},{10,11... | collective-permute-start | bytes 4718600 | tf_op jit(solution)/shard_map/ppermute | solution.py:716
  32.3 16.8 %all-to-all-start = ((bf16[16,16,896]{2,1,0:T(8,128)(2,1)}), bf16[16,16,896]{2,1,0:T(8,128)(2,1)S(1)}, u32[]{:S(2)}, u32[]{:S(2)}) async-start(bf16[16,16,896]{2,1,0:T(8,128)(2,1)} %shard_map.100), calls=%async_computation | async-start | bytes 917504 | tf_op jit(solution)/shard_map/all_to_all | solution.py:656

commit v4 on v3

--- a/solution.py
+++ b/solution.py
@@ -564,10 +564,11 @@
     up_video(dims, ready, x_ref, all_ref, new_ref, gain_ref, t_ref, m0_ref, m2_ref, store)
 
 
-def place_kernel(share, x_ref, out_ref, line):
+def place_kernel(share, x_ref, out_any, line, out_ref, sems):
     devices = x_ref.shape[0]
     blocks = LANES // share
     cols = x_ref.shape[1]
+    outs = []
     for a in range(devices // blocks):
         pieces = swap_blocks(
             [x_ref[a * blocks + k].astype(jnp.float32) for k in range(blocks)], share
@@ -576,9 +577,15 @@
             slot = a * (blocks // 2) + half
             for q in range(2):
                 line[slot, pl.ds(q, cols, stride=2), :] = pieces[2 * half + q]
-            out_ref[half // 2, half % 2, :, a * LANES : (a + 1) * LANES] = line[slot].astype(
-                out_ref.dtype
+            out_ref[a, half // 2, half % 2] = line[slot].astype(out_ref.dtype)
+        outs.append(
+            pltpu.make_async_copy(
+                out_ref.at[a], out_any.at[:, :, :, a * LANES : (a + 1) * LANES], sems.at[a]
             )
+        )
+        outs[-1].start()
+    for copy in outs:
+        copy.wait()
 
 
 def fits(mesh, shapes):
@@ -727,11 +734,16 @@
     return call(
         functools.partial(place_kernel, share),
         shape((frames, 2 * own, 2 * cols, chan), bf16),
-        [pltpu.VMEM((2 * count // 2, 2 * cols, LANES), f32)],
+        [
+            pltpu.VMEM((2 * count // 2, 2 * cols, LANES), f32),
+            pltpu.VMEM((chan // LANES, frames, 2 * own, 2 * cols, LANES), bf16),
+            pltpu.SemaphoreType.DMA((chan // LANES,)),
+        ],
         8,
         10**6,
         10**6,
         (pltpu.VMEM,),
+        pltpu.HBM,
     )(swapped)
 
 

time: 72.8 us -> 72.7 us (level)
  no operation moved by 1% of the time
where the time goes in v4:
time: 72.7 us; the launch traced here: 72.3 us
  blocking collectives  30.9 us (43%)
  Pallas kernels  21.1 us (29%)
  waiting for transfers between devices  13 us (18%)
  starting transfers between devices  3.9 us (5%)
  local copies, waits for them, and re-layouts  3.27 us (4%)
    all_to_all x1, blocking collectives, whole_video(): swapped = lax.all_to_all(decoded, ('grp', 'row'), 0, 0, tiled=True)  15.6 us
    all_to_all x1, blocking collectives, whole_video(): cells = lax.all_to_all(cells, ('grp', 'row'), 0, 0, tiled=True)  15.3 us
    all_to_all x1, waiting for transfers between devices, whole_video(): weights = lax.all_to_all(packed, 'row', 0, 0, tiled=True)  13 us
    pallas_call x1, Pallas kernels, whole_video(): middle(cells, jnp.asarray(spread, bf16), w_in.reshape(3 * depth, chan), g...  10.6 us
    all_to_all x1, starting transfers between devices, whole_video(): weights = lax.all_to_all(packed, 'row', 0, 0, tiled=True)  3.57 us
    pallas_call x1, Pallas kernels, whole_video(): call(functools.partial(far_kernel, dims), shape((2 * count, cols, LANES),...  3.38 us
    pallas_call x1, Pallas kernels, whole_video(): near_out, fold_all, fold_new = first(weights, added, gain)  2.86 us
    pallas_call x1, Pallas kernels, whole_video(): packed = pack(pltpu.with_memory_space_constraint(w_up, pltpu.HBM))  2.62 us
  transfers between devices with their start and end apart: 2, of which 1 were waited for; matrix products, arithmetic and copies ran while one was open for 0% of the time, Pallas kernels for 8%

profile of v4, /device:TPU:0, one launch (start us, length us, event | category | flops | bytes accessed | tf_op | source)
XLA Modules:
  0.0 72.3 jit_solution(1935031315840914595)
XLA Ops:
  0.0 0.7 fusion
  0.7 0.1 pad_maximum_fusion
  0.8 15.3 %all_to_all.15.z_ref = bf16[32,16,128]{2,1,0:T(8,128)(2,1)S(1)} all-to-all(bf16[32,16,128]{2,1,0:T(8,128)(2,1)S(1)} %broadcast_in_dim.3), channel_id=1, replica_groups=mesh['grp'=2,'row'=16] {'grp','row'}, dimensions={0} | all-to-all | bytes 262144 | tf_op jit(solution)/shard_map/all_to_all | solution.py:645
  16.2 0.0 copy-start.1
  16.2 1.0 %copy-done.1 = bf16[27,16,512]{2,1,0:T(8,128)(2,1)S(1)} copy-done((bf16[27,16,512]{2,1,0:T(8,128)(2,1)S(1)}, bf16[27,16,512]{2,1,0:T(8,128)(2,1)}, u32[]{:S(2)}) %copy-start.1) | copy-done | bytes 442392
  17.2 0.0 copy-start.2
  17.2 0.7 copy-done.2
  17.8 0.0 copy-start.3
  17.8 0.8 %copy-done.3 = bf16[128,144]{1,0:T(8,128)(2,1)S(1)} copy-done((bf16[128,144]{1,0:T(8,128)(2,1)S(1)}, bf16[128,144]{1,0:T(8,128)(2,1)}, u32[]{:S(2)}) %copy-start.3) | copy-done | bytes 36888
  18.7 10.6 %shard_map.101.x_ref = bf16[1536,512]{1,0:T(8,128)(2,1)S(1)} custom-call(bf16[32,16,128]{2,1,0:T(8,128)(2,1)S(1)} %all_to_all.15.z_ref, bf16[128,144]{1,0:T(8,128)(2,1)S(1)} %copy-done.3, bf16[432,512]{1,0:T(8,128)(2,1)S(1)} %bitcast.13, f32[1,512]{1,0:T(1,128)S(1)} %bitcast.14, bf16[512,512]{1,0:T(8,128)(2,1)} %wq_any.1, bf16[512,512]{1,0:T(8,128)(2,1)} %wk_any.1, ...), custom_call_target="tpu_custom_call" | custom-call | flops 7000000000 | bytes 6000000 | tf_op jit(solution)/shard_map/pallas_call | solution.py:688
  29.3 0.0 copy-start
  29.3 0.3 collective-permute-start
  29.6 2.6 %shard_map.100 = bf16[16,16,896]{2,1,0:T(8,128)(2,1)} custom-call(bf16[27,32,512]{2,1,0:T(8,128)(2,1)} %w_any.1), custom_call_target="tpu_custom_call" | custom-call | flops 1000000 | bytes 2000000 | tf_op jit(solution)/shard_map/pallas_call | solution.py:662
  32.3 3.6 %all-to-all-start = ((bf16[16,16,896]{2,1,0:T(8,128)(2,1)}), bf16[16,16,896]{2,1,0:T(8,128)(2,1)S(1)}, u32[]{:S(2)}, u32[]{:S(2)}) async-start(bf16[16,16,896]{2,1,0:T(8,128)(2,1)} %shard_map.100), calls=%async_computation | async-start | bytes 917504 | tf_op jit(solution)/shard_map/all_to_all | solution.py:663
  35.9 0.0 copy-done
  35.9 0.2 shard_map.102.gain_ref
  36.1 13.0 %all-to-all-done = bf16[16,16,896]{2,1,0:T(8,128)(2,1)S(1)} async-done(((bf16[16,16,896]{2,1,0:T(8,128)(2,1)}), bf16[16,16,896]{2,1,0:T(8,128)(2,1)S(1)}, u32[]{:S(2)}, u32[]{:S(2)}) %all-to-all-start) | async-done | bytes 458784 | tf_op jit(solution)/shard_map/all_to_all | solution.py:663
  49.0 2.9 %shard_map.103 = (bf16[16,48,128]{2,1,0:T(8,128)(2,1)S(1)}, bf16[512,512]{1,0:T(8,128)(2,1)S(1)}, bf16[512,512]{1,0:T(8,128)(2,1)S(1)}) custom-call(bf16[256,896]{1,0:T(8,128)(2,1)S(1)} %bitcast.11, bf16[1536,512]{1,0:T(8,128)(2,1)S(1)} %shard_map.101.x_ref, f32[8,128]{1,0:T(8,128)S(1)} %shard_map.102.gain_ref), custom_call_target="tpu_custom_call" | custom-call | flops 2000000000 | bytes 3000000 | tf_op jit(solution)/shard_map/pallas_call | solution.py:722
  51.9 0.0 collective-permute-done.x_any
  51.9 3.4 %shard_map.104 = bf16[32,48,128]{2,1,0:T(8,128)(2,1)S(1)} custom-call(bf16[16,48,128]{2,1,0:T(8,128)(2,1)S(1)} %get-tuple-element.8.near_ref, bf16[1536,512]{1,0:T(8,128)(2,1)} %collective-permute-done.x_any, bf16[512,512]{1,0:T(8,128)(2,1)S(1)} %get-tuple-element.9.all_ref, bf16[512,512]{1,0:T(8,128)(2,1)S(1)} %get-tuple-element.10.new_ref, ...), custom_call_target="tpu_custom_call" | custom-call | flops 2000000000 | bytes 3000000 | tf_op jit(solution)/shard_map/pallas_call | solution.py:724
  55.3 15.6 %all_to_all.16.x_ref = bf16[32,48,128]{2,1,0:T(8,128)(2,1)S(1)} all-to-all(bf16[32,48,128]{2,1,0:T(8,128)(2,1)S(1)} %shard_map.104), channel_id=1, replica_groups=mesh['grp'=2,'row'=16] {'grp','row'}, dimensions={0} | all-to-all | bytes 786432 | tf_op jit(solution)/shard_map/all_to_all | solution.py:733
  70.9 1.4 %shard_map.105 = bf16[2,2,96,512]{3,2,1,0:T(8,128)(2,1)} custom-call(bf16[32,48,128]{2,1,0:T(8,128)(2,1)S(1)} %all_to_all.16.x_ref), custom_call_target="tpu_custom_call" | custom-call | flops 1000000 | bytes 1000000 | tf_op jit(solution)/shard_map/pallas_call | solution.py:734
  (1 shorter events, 0.0 us)
Async XLA Ops:
  16.2 1.0 %copy-start.1 = (bf16[27,16,512]{2,1,0:T(8,128)(2,1)S(1)}, bf16[27,16,512]{2,1,0:T(8,128)(2,1)}, u32[]{:S(2)}) copy-start(bf16[27,16,512]{2,1,0:T(8,128)(2,1)} %param.11) | copy-start | bytes 1327108
  17.2 0.7 copy-start.2
  17.8 0.8 %copy-start.3 = (bf16[128,144]{1,0:T(8,128)(2,1)S(1)}, bf16[128,144]{1,0:T(8,128)(2,1)}, u32[]{:S(2)}) copy-start(bf16[128,144]{1,0:T(8,128)(2,1)} %constant.5.clone.spread_ref) | copy-start | bytes 110596
  29.3 6.6 %copy-start = (f32[512]{0:T(512)S(1)}, f32[512]{0:T(512)}, u32[]{:S(2)}) copy-start(f32[512]{0:T(512)} %param.17) | copy-start | bytes 6148
  29.3 22.6 %collective-permute-start = (bf16[1536,512]{1,0:T(8,128)(2,1)S(1)}, bf16[1536,512]{1,0:T(8,128)(2,1)}, u32[]{:S(2)}, u32[]{:S(2)}) collective-permute-start(bf16[1536,512]{1,0:T(8,128)(2,1)S(1)} %shard_map.101.x_ref), channel_id=1, source_target_pairs={{0,1},{1,0},{2,3},{3,2},{4,5},{5,4},{6,7},{7,6},{8,9},{9,8},{10,11... | collective-permute-start | bytes 4718600 | tf_op jit(solution)/shard_map/ppermute | solution.py:723
  32.3 16.8 %all-to-all-start = ((bf16[16,16,896]{2,1,0:T(8,128)(2,1)}), bf16[16,16,896]{2,1,0:T(8,128)(2,1)S(1)}, u32[]{:S(2)}, u32[]{:S(2)}) async-start(bf16[16,16,896]{2,1,0:T(8,128)(2,1)} %shard_map.100), calls=%async_computation | async-start | bytes 917504 | tf_op jit(solution)/shard_map/all_to_all | solution.py:663
